TPU v7x, 32 devices: a whole 2x2x4 slice. The times are simulated.
32 devices in a mesh: grp: 2 (over x), seq: 4 (over y, core), sub: 4 (over z).
Axes of the slice: x: 2, y: 2, z: 4, core: 2. Of those that a mesh axis runs over, the one named last changes fastest.
Arguments:
- query_rows: bfloat16 [8, 512, 2048], P(('grp', 'sub'), 'seq'), parts along dimension 0, may hold values from -9 to 9
- key_rows: bfloat16 [8, 512, 256], P(('grp', 'sub'), 'seq'), parts along dimension 0, may hold values from -4 to 4
- value_rows: bfloat16 [8, 512, 256], P(('grp', 'sub'), 'seq'), parts along dimension 0, may hold values from -6 to 6
- residual_in: bfloat16 [8, 512, 2048], P(('grp', 'sub'), 'seq'), parts along dimension 0, may hold values from -6 to 6
- out_proj: bfloat16 [2048, 2048], P('seq'), may hold values from -0.5 to 0.5
- norm_gain: bfloat16 [2048], replicated, may hold values from 0.099609375 to 1.8984375
- expert_ids: int32 [8, 512, 8], P(('grp', 'sub'), 'seq'), parts along dimension 0, may hold values from 0 to 15, all different within a row; in each aligned block of 128 rows (0 to 127, 128 to 255, ..., all dimensions but the last counted through in order) at most 80 rows name the same one
- gate_weights: bfloat16 [8, 512, 8], P(('grp', 'sub'), 'seq'), parts along dimension 0, may hold values from 0.049804688 to 1
- expert_gate: bfloat16 [16, 2048, 768], P(('seq', 'sub')), may hold values from -0.125 to 0.125
- expert_up: bfloat16 [16, 2048, 768], P(('seq', 'sub')), may hold values from -0.125 to 0.125
- expert_down: bfloat16 [16, 768, 2048], P(('seq', 'sub')), may hold values from -0.21875 to 0.21875
Outputs:
- layer_out: bfloat16 [8, 512, 2048], P(('grp', 'sub'), 'seq'), parts along dimension 0
There are 2 independent parts, one for each index of `grp`. A program takes and returns all parts, laid end to end along the dimension named above; an argument that names none is the same for every part. Nothing has to cross between parts.
Inputs may be any that keep to these rules, and one draw needn't show every extreme that they name: `expert_ids`: A row names 8 different experts. In each aligned block of 128 rows (the rows of one device) no expert is named by more than 80 rows, a bound that some block reaches.
All inputs are finite; a program needn't handle non-finite values.
Results may differ from a plain program's by a relative error of at most 0.013.
Values may be sent and summed in bfloat16 or wider, within the bound.
A program may use at most 128 MiB of HBM per device.

v0:
```python
import jax
import jax.numpy as jnp
from jax import lax
from jax.sharding import PartitionSpec as P

D = 2048
HD = 128
QH = 16
KVH = 2


def attend_head(queries, keys_one, values_one, block):
    length = queries.shape[0]
    scale = 1.0 / queries.shape[1] ** 0.5
    pieces = []
    for part_index in range(length // block):
        stop = (part_index + 1) * block
        rows_here = queries[part_index * block : stop]
        scores = (
            jnp.einsum("qd,kd->qk", rows_here, keys_one[:stop], preferred_element_type=jnp.float32)
            * scale
        )
        row_pos = part_index * block + jnp.arange(block, dtype=jnp.int32)
        col_pos = jnp.arange(stop, dtype=jnp.int32)
        scores = jnp.where(row_pos[:, None] >= col_pos[None, :], scores, -1e30)
        peak = jnp.max(scores, axis=1, keepdims=True)
        weights = jnp.exp(scores - peak)
        probs = (weights / jnp.sum(weights, axis=1, keepdims=True)).astype(jnp.bfloat16)
        pieces.append(
            jnp.dot(probs, values_one[:stop], preferred_element_type=jnp.float32).astype(
                jnp.bfloat16
            )
        )
    return jnp.concatenate(pieces, axis=0)


def rank_in_expert(flat_ids, experts):
    items = flat_ids.shape[0]
    width = 128
    n_parts = items // width
    onehot = (
        (flat_ids[:, None] == jnp.arange(experts, dtype=jnp.int32)[None, :])
        .astype(jnp.bfloat16)
        .reshape(n_parts, width, experts)
    )
    lower = (
        jnp.arange(width, dtype=jnp.int32)[:, None] > jnp.arange(width, dtype=jnp.int32)[None, :]
    ).astype(jnp.bfloat16)
    within = jnp.einsum("ij,bje->bie", lower, onehot, preferred_element_type=jnp.float32)
    part_counts = jnp.sum(onehot.astype(jnp.float32), axis=1)
    earlier = jnp.cumsum(part_counts, axis=0) - part_counts
    ranks = jnp.sum((within + earlier[:, None, :]) * onehot.astype(jnp.float32), axis=2)
    return ranks.reshape(items).astype(jnp.int32)


def per_device(
    query_rows,
    key_rows,
    value_rows,
    residual_in,
    out_proj,
    norm_gain,
    expert_ids,
    gate_weights,
    expert_gate,
    expert_up,
    expert_down,
):
    tokens = query_rows.shape[1]
    n_seq = lax.axis_size("seq")
    n_sub = lax.axis_size("sub")
    heads_here = QH // n_seq
    group = QH // KVH
    query_local = lax.all_to_all(query_rows, "seq", split_axis=2, concat_axis=1, tiled=True)
    key_full, value_full = (
        lax.all_gather(key_rows, "seq", axis=1, tiled=True),
        lax.all_gather(value_rows, "seq", axis=1, tiled=True),
    )
    first_head = lax.axis_index("seq") * heads_here
    key_list = []
    value_list = []
    for head in range(heads_here):
        kv_start = (first_head + head) // group * HD
        key_list.append(lax.dynamic_slice_in_dim(key_full[0], kv_start, HD, 1))
        value_list.append(lax.dynamic_slice_in_dim(value_full[0], kv_start, HD, 1))
    length = query_local.shape[1]
    block = min(length, max(512, length // 8))
    outputs = [
        attend_head(
            query_local[0, :, head * HD : (head + 1) * HD], key_list[head], value_list[head], block
        )
        for head in range(heads_here)
    ]
    head_block = jnp.concatenate(outputs, axis=1)[None]
    attended = lax.all_to_all(head_block, "seq", split_axis=1, concat_axis=2, tiled=True)[0]
    projected = jnp.dot(
        attended,
        lax.all_gather(out_proj, "seq", axis=0, tiled=True),
        preferred_element_type=jnp.float32,
    )
    hidden = (residual_in[0].astype(jnp.float32) + projected).astype(jnp.bfloat16)
    wide = hidden.astype(jnp.float32)
    normed = (
        wide
        * lax.rsqrt(jnp.mean(wide * wide, axis=1, keepdims=True) + 1e-06)
        * norm_gain.astype(jnp.float32)
    ).astype(jnp.bfloat16)
    topk = expert_ids.shape[2]
    experts = n_seq * n_sub
    cap = max(2, (5 * tokens * topk + 4 * experts - 1) // (4 * experts))
    flat_ids = expert_ids[0].reshape(-1)
    items = flat_ids.shape[0]
    ranks = rank_in_expert(flat_ids, experts)
    slot_of = flat_ids * cap + ranks
    slots_out = experts * cap
    item_of_slot = (
        jnp.full((slots_out,), items, jnp.int32).at[slot_of].set(jnp.arange(items, dtype=jnp.int32))
    )
    padded_rows = jnp.concatenate([normed, jnp.zeros((1, D), jnp.bfloat16)], axis=0)
    padded_gates = jnp.concatenate(
        [gate_weights[0].reshape(-1), jnp.zeros((1,), jnp.bfloat16)], axis=0
    )
    token_of_slot = jnp.where(item_of_slot < items, item_of_slot // topk, tokens)
    send_rows = padded_rows[token_of_slot].reshape(experts, cap, D)
    send_gates = padded_gates[item_of_slot].reshape(experts, cap)
    recv_rows, recv_gates = (
        lax.all_to_all(send_rows, ("seq", "sub"), split_axis=0, concat_axis=0, tiled=True),
        lax.all_to_all(send_gates, ("seq", "sub"), split_axis=0, concat_axis=0, tiled=True),
    )
    slots_in = experts * cap
    valid = recv_gates > 0
    counts = jnp.sum(valid.astype(jnp.int32), axis=1)
    offsets = jnp.cumsum(counts) - counts
    dest = jnp.where(
        valid, offsets[:, None] + jnp.arange(cap, dtype=jnp.int32)[None, :], slots_in
    ).reshape(-1)
    source_of = (
        jnp.full((slots_in + 1,), slots_in, jnp.int32)
        .at[dest]
        .set(jnp.arange(slots_in, dtype=jnp.int32))[:slots_in]
    )
    compact_rows = jnp.concatenate(
        [recv_rows.reshape(slots_in, D), jnp.zeros((1, D), jnp.bfloat16)], axis=0
    )[source_of]
    compact_gates = jnp.concatenate(
        [recv_gates.reshape(-1), jnp.zeros((1,), jnp.bfloat16)], axis=0
    )[source_of].astype(jnp.float32)
    filled = jnp.sum(counts)
    n_blocks = (filled + slots_in - 1) // slots_in
    w_gate = expert_gate[0]
    w_up = expert_up[0]
    w_down = expert_down[0]

    def expert_block(index, results):
        gate_proj = jnp.dot(compact_rows, w_gate, preferred_element_type=jnp.float32)
        up_proj = jnp.dot(compact_rows, w_up, preferred_element_type=jnp.float32)
        inner = (jax.nn.silu(gate_proj) * up_proj).astype(jnp.bfloat16)
        weighted = (
            jnp.dot(inner, w_down, preferred_element_type=jnp.float32) * compact_gates[:, None]
        )
        return weighted.astype(jnp.bfloat16)

    results = lax.fori_loop(0, n_blocks, expert_block, jnp.zeros((slots_in, D), jnp.bfloat16))
    returned = jnp.concatenate([results, jnp.zeros((1, D), jnp.bfloat16)], axis=0)[dest].reshape(
        experts, cap, D
    )
    back = lax.all_to_all(
        returned, ("seq", "sub"), split_axis=0, concat_axis=0, tiled=True
    ).reshape(slots_out, D)
    gathered = back[slot_of].reshape(tokens, topk, D).astype(jnp.float32)
    mixture = jnp.sum(gathered, axis=1)
    return (wide + mixture).astype(jnp.bfloat16)[None]


def solution(mesh):
    placed = (
        P(("grp", "sub"), "seq", None),
        P(("grp", "sub"), "seq", None),
        P(("grp", "sub"), "seq", None),
        P(("grp", "sub"), "seq", None),
        P("seq", None),
        P(),
        P(("grp", "sub"), "seq", None),
        P(("grp", "sub"), "seq", None),
        P(("seq", "sub"), None, None),
        P(("seq", "sub"), None, None),
        P(("seq", "sub"), None, None),
    )
    return jax.shard_map(
        per_device,
        mesh=mesh,
        in_specs=placed,
        out_specs=P(("grp", "sub"), "seq", None),
        check_vma=False,
    )
```

profile of v0, /device:TPU:0, one launch (start us, length us, event | category | flops | bytes accessed | tf_op | source)
XLA Modules:
  0.0 475.5 jit_solution(11727438130950992658)
XLA Ops:
  6.6 0.7 all-gather.2.cloned.1.call-update
  7.3 3.7 copy.33
  11.0 0.6 broadcast.193
  11.6 13.3 %reduce.9 = bf16[2048,128]{1,0:T(8,128)(2,1)} reduce(bf16[2048,1,128]{2,1,0:T(2,128)(2,1)} %bitcast.127, bf16[]{:T(256)} %broadcast.193), dimensions={1}, to_apply=%bitcast.95.reduce_sub_computation | reduce | bytes 1048578
  24.9 2.0 reshape.276
  26.9 4.3 all-to-all-start
  31.2 0.1 copy.37
  31.3 0.1 reshape_squeeze.4
  32.0 0.2 fusion.18
  32.2 18.7 %all_gather.9 = bf16[1,512,256]{2,1,0:T(8,128)(2,1)} all-gather(bf16[1,128,256]{2,1,0:T(8,128)(2,1)S(1)} %copy-done.6), channel_id=1, replica_groups=mesh['grp'=2,'seq'=4,'sub'=4] {'seq'}, dimensions={1}, use_global_device_ids=true | all-gather | bytes 327680 | tf_op jit(solution)/shard_map/all_gather | solution.py:76
  50.9 8.2 %all_gather.10 = bf16[1,512,256]{2,1,0:T(8,128)(2,1)S(1)} all-gather(bf16[1,128,256]{2,1,0:T(8,128)(2,1)S(1)} %copy-done.7), channel_id=1, replica_groups=mesh['grp'=2,'seq'=4,'sub'=4] {'seq'}, dimensions={1}, use_global_device_ids=true | all-gather | bytes 327680 | tf_op jit(solution)/shard_map/all_gather | solution.py:77
  59.1 3.5 reshape.277
  62.6 2.1 copy.42
  64.7 2.1 copy.34
  66.8 1.3 fusion.62
  68.1 0.2 fusion.22
  68.3 1.3 fusion.63
  69.6 0.2 fusion.21
  69.8 1.3 fusion.64
  71.1 0.2 fusion.20
  71.3 1.2 fusion.65
  72.5 0.2 fusion.19
  72.7 0.3 convolution_convert_fusion
  73.0 0.3 convolution_convert_fusion.1
  73.4 0.3 convolution_convert_fusion.2
  73.8 0.3 convolution_convert_fusion.3
  74.1 0.8 maximum_bitcast_fusion
  74.9 3.6 copy.35
  78.5 5.5 %reduce.10 = bf16[512,512]{1,0:T(8,128)(2,1)} reduce(bf16[512,1,512]{2,1,0:T(2,128)(2,1)} %bitcast.126, bf16[]{:T(256)} %broadcast.193), dimensions={1}, to_apply=%bitcast.97.reduce_sub_computation | reduce | bytes 1048578
  84.1 2.3 reshape.278
  86.4 4.1 all-to-all-start.1
  90.5 4.3 scatter_custom_fusion
  94.9 8.0 %gather_fusion = bf16[1280]{0:T(1024)(128)(2,1)S(1)} fusion(bf16[1025]{0:T(1024)(128)(2,1)S(1)} %pad_maximum_fusion, s32[2048]{0:T(1024)S(1)} %get-tuple-element.173), kind=kCustom, calls=%fused_computation | custom fusion | bytes 10240 | tf_op jit(solution)/shard_map/gather | solution.py:125
  102.9 0.7 all_to_all.47
  103.6 7.1 %all-to-all-start.2 = ((bf16[16,1,80]{2,1,0:T(2,128)(2,1)}), bf16[16,1,80]{2,1,0:T(2,128)(2,1)S(1)}, u32[]{:S(2)}, u32[]{:S(2)}) async-start(bf16[16,1,80]{2,1,0:T(2,128)(2,1)} %all_to_all.47), calls=%async_computation.2 | async-start | bytes 16384 | tf_op jit(solution)/shard_map/all_to_all | solution.py:128
  110.7 3.5 reshape.279
  114.2 2.1 copy.43
  116.4 2.1 copy.36
  118.5 4.9 %multiply_reduce_fusion = (f32[128]{0:T(128)S(1)}, f32[128,2048]{1,0:T(8,128)S(1)}) fusion(bf16[128,2048]{0,1:T(8,128)(2,1)} %bitcast.128, bf16[2048,2048]{1,0:T(8,128)(2,1)} %all-gather.2.cloned.1.call-done, bf16[1,128,2048]{2,1,0:T(8,128)(2,1)} %param.16), kind=kOutput, calls=%fused_computation.42 | convolution fusion | flops 1075314560 | bytes 10486272 | tf_op jit(solution)/shard_map/dot_general | solution.py:96
  123.4 1.0 copy-done.2
  124.4 0.2 multiply_convert_fusion.1
  124.6 0.9 concatenate.21
  125.4 11.9 %gather_fusion.2 = bf16[1280,2048]{1,0:T(8,128)(2,1)} fusion(bf16[129,2048]{1,0:T(8,128)(2,1)} %concatenate.21, s32[2048]{0:T(1024)S(1)} %get-tuple-element.172), kind=kCustom, calls=%fused_computation.2 | custom fusion | bytes 10490880 | tf_op jit(solution)/shard_map/gather | solution.py:124
  137.4 6.1 %all-to-all-start.3 = ((bf16[16,80,2048]{2,1,0:T(8,128)(2,1)}), bf16[16,80,2048]{2,1,0:T(8,128)(2,1)}, u32[]{:S(2)}, u32[]{:S(2)}) async-start(bf16[16,80,2048]{2,1,0:T(8,128)(2,1)} %bitcast.122), calls=%async_computation.3 | async-start | bytes 10485760 | tf_op jit(solution)/shard_map/all_to_all | solution.py:127
  143.5 0.9 fusion.48
  145.5 0.1 reduce.5
  145.9 5.5 %scatter_custom_fusion.1 = s32[1281]{0:T(1024)S(1)} fusion(s32[1280]{0:T(1024)S(1)} %fusion.47, s32[1280]{0:T(1024)S(1)} %iota.44, s32[]{:T(128)} %constant.125.clone.1), kind=kCustom, calls=%fused_computation.109 | custom fusion | bytes 5128 | tf_op jit(solution)/shard_map/scatter | solution.py:140
  151.4 8.0 %gather_fusion.1 = bf16[1280]{0:T(1024)(128)(2,1)S(1)} fusion(bf16[1281]{0:T(1024)(128)(2,1)S(1)} %pad_maximum_fusion.1, s32[2048]{0:T(1024)S(1)} %pad_clamp_fusion.2), kind=kCustom, calls=%fused_computation.1 | custom fusion | bytes 10240 | tf_op jit(solution)/shard_map/gather | solution.py:145
  159.4 100.9 %all-to-all-done.3 = bf16[16,80,2048]{2,1,0:T(8,128)(2,1)} async-done(((bf16[16,80,2048]{2,1,0:T(8,128)(2,1)}), bf16[16,80,2048]{2,1,0:T(8,128)(2,1)}, u32[]{:S(2)}, u32[]{:S(2)}) %all-to-all-start.3) | async-done | bytes 5242912 | tf_op jit(solution)/shard_map/all_to_all | solution.py:127
  260.3 5.7 %concatenate.22 = bf16[1281,2048]{1,0:T(8,128)(2,1)} pad(bf16[1280,2048]{1,0:T(8,128)(2,1)} %bitcast.28, bf16[]{:T(256)} %constant.121.clone.1), padding=0_1x0_0 | pad | bytes 10489858 | tf_op jit(solution)/shard_map/concatenate | solution.py:142
  266.0 14.0 %gather_fusion.3 = bf16[1280,2048]{1,0:T(8,128)(2,1)} fusion(bf16[1281,2048]{1,0:T(8,128)(2,1)} %concatenate.22, s32[2048]{0:T(1024)S(1)} %pad_clamp_fusion.2), kind=kCustom, calls=%fused_computation.3 | custom fusion | bytes 10490880 | tf_op jit(solution)/shard_map/gather | solution.py:142
  280.0 7.2 %fusion.4 = f32[1280,768]{1,0:T(8,128)S(1)} fusion(bf16[1280,2048]{1,0:T(8,128)(2,1)} %gather_fusion.3, bf16[1,2048,768]{2,1,0:T(8,128)(2,1)} %param.21), kind=kOutput, calls=%fused_computation.15 | convolution fusion | flops 4026531840 | bytes 12320768 | tf_op jit(solution)/shard_map/while/body/dot_general | solution.py:155
  287.2 4.8 %fusion = bf16[1280,768]{1,0:T(8,128)(2,1)S(1)} fusion(bf16[1280,2048]{1,0:T(8,128)(2,1)S(1)} %copy-done.4, f32[1280,768]{1,0:T(8,128)S(1)} %fusion.4, bf16[1,2048,768]{2,1,0:T(8,128)(2,1)S(1)} %copy-done.11), kind=kOutput, calls=%fused_computation.11 | convolution fusion | flops 4032430080 | bytes 14286848 | tf_op jit(solution)/shard_map/while/body/dot_general | solution.py:156
  292.1 6.9 %fusion.1 = f32[1280,2048]{1,0:T(8,128)} fusion(bf16[1280,768]{1,0:T(8,128)(2,1)S(1)} %fusion, bf16[1,768,2048]{2,1,0:T(8,128)(2,1)S(1)} %copy-done), kind=kOutput, calls=%fused_computation.12 | convolution fusion | flops 4026531840 | bytes 15597568 | tf_op jit(solution)/shard_map/while/body/dot_general | solution.py:159
  299.0 3.0 broadcast_in_dim.30
  302.0 7.2 %while.14 = (s32[]{:T(128)}, bf16[1280,2048]{1,0:T(8,128)(2,1)}, s32[]{:T(128)}, f32[1280]{0:T(1024)S(1)}, f32[1280,2048]{1,0:T(8,128)}, /*index=5*/s32[]{:T(128)}) while((s32[]{:T(128)}, bf16[1280,2048]{1,0:T(8,128)(2,1)}, s32[]{:T(128)}, f32[1280]{0:T(1024)S(1)}, f32[1280,2048]{1,0:T(8,128)}, /*index=5*/s32[]{:T(128)}) %tuple.40), condition=%wide.region_18.19_spmd, body=%wide.region_17.18_spmd.sunk | while | flops 5242882 | bytes 15733829 | solution.py:163
  302.0 7.0 %multiply_convert_fusion.3 = bf16[1280,2048]{1,0:T(8,128)(2,1)} fusion(f32[1280,2048]{1,0:T(8,128)} %get-tuple-element.220, f32[1280]{0:T(1024)S(1)} %get-tuple-element.219), kind=kLoop, calls=%fused_computation.8.clone.1 | loop fusion | flops 5242880 | bytes 15733760 | tf_op jit(solution)/shard_map/while/body/convert_element_type | solution.py:161
  309.2 5.7 %concatenate.23 = bf16[1281,2048]{1,0:T(8,128)(2,1)} pad(bf16[1280,2048]{1,0:T(8,128)(2,1)} %get-tuple-element.147, bf16[]{:T(256)} %constant.121.clone.1), padding=0_1x0_0 | pad | bytes 10489858 | tf_op jit(solution)/shard_map/concatenate | solution.py:164
  314.8 14.0 %gather_fusion.4 = bf16[1280,2048]{1,0:T(8,128)(2,1)} fusion(bf16[1281,2048]{1,0:T(8,128)(2,1)} %concatenate.23, s32[2048]{0:T(1024)S(1)} %pad_clamp_fusion), kind=kCustom, calls=%fused_computation.4 | custom fusion | bytes 10490880 | tf_op jit(solution)/shard_map/gather | solution.py:164
  328.8 4.6 all-to-all-start.4
  333.4 116.7 %all-to-all-done.4 = bf16[16,80,2048]{2,1,0:T(8,128)(2,1)} async-done(((bf16[16,80,2048]{2,1,0:T(8,128)(2,1)}), bf16[16,80,2048]{2,1,0:T(8,128)(2,1)}, u32[]{:S(2)}, u32[]{:S(2)}) %all-to-all-start.4) | async-done | bytes 5242912 | tf_op jit(solution)/shard_map/all_to_all | solution.py:167
  450.2 12.2 %gather_fusion.5 = bf16[1024,2048]{1,0:T(8,128)(2,1)} fusion(bf16[1280,2048]{1,0:T(8,128)(2,1)} %bitcast.33, s32[1024]{0:T(1024)S(1)} %broadcast_clamp_fusion), kind=kCustom, calls=%fused_computation.5 | custom fusion | bytes 8392704 | tf_op jit(solution)/shard_map/gather | solution.py:170
  462.4 5.1 %convert_reduce_fusion = f32[128,2048]{1,0:T(8,128)S(1)} fusion(bf16[1024,2048]{1,0:T(8,128)(2,1)} %gather_fusion.5), kind=kLoop, calls=%fused_computation.9 | loop fusion | flops 3932160 | bytes 5242880 | tf_op jit(solution)/shard_map/reduce_sum | solution.py:171
  467.5 0.9 fusion.23
  (61 shorter events, 1.3 us)
Async XLA Ops:
  6.5 285.5 %copy-start = (bf16[1,768,2048]{2,1,0:T(8,128)(2,1)S(1)}, bf16[1,768,2048]{2,1,0:T(8,128)(2,1)}, u32[]{:S(2)}) copy-start(bf16[1,768,2048]{2,1,0:T(8,128)(2,1)} %param.23) | copy-start | bytes 9437188
  6.5 24.6 %copy-start.10 = (bf16[1,128,8]{1,2,0:T(8,128)(2,1)S(1)}, bf16[1,128,8]{1,2,0:T(8,128)(2,1)}, u32[]{:S(2)}) copy-start(bf16[1,128,8]{1,2,0:T(8,128)(2,1)} %param.20) | copy-start | bytes 6148
  6.5 24.9 %copy-start.8 = (s32[1,128,8]{1,2,0:T(8,128)S(1)}, s32[1,128,8]{1,2,0:T(8,128)}, u32[]{:S(2)}) copy-start(s32[1,128,8]{1,2,0:T(8,128)} %param.19) | copy-start | bytes 12292
  6.5 25.6 %copy-start.6 = (bf16[1,128,256]{2,1,0:T(8,128)(2,1)S(1)}, bf16[1,128,256]{2,1,0:T(8,128)(2,1)}, u32[]{:S(2)}) copy-start(bf16[1,128,256]{2,1,0:T(8,128)(2,1)} %param.14) | copy-start | bytes 196612
  6.5 44.3 %copy-start.7 = (bf16[1,128,256]{2,1,0:T(8,128)(2,1)S(1)}, bf16[1,128,256]{2,1,0:T(8,128)(2,1)}, u32[]{:S(2)}) copy-start(bf16[1,128,256]{2,1,0:T(8,128)(2,1)} %param.15) | copy-start | bytes 196612
  6.5 111.9 %all-gather.2.cloned.1.call-start = ((), (), s32[]{:S(2)}) async-start(), calls=%async_computation.5 | async-start | bytes 10485760 | tf_op jit(solution)/shard_map/all_gather | solution.py:98
  26.9 32.2 %all-to-all-start = ((bf16[4,2,32768]{2,1,0:T(2,128)(2,1)}), bf16[4,2,32768]{2,1,0:T(2,128)(2,1)}, u32[]{:S(2)}, u32[]{:S(2)}) async-start(bf16[4,2,32768]{2,1,0:T(2,128)(2,1)} %reshape.276), calls=%async_computation | async-start | bytes 1048576 | tf_op jit(solution)/shard_map/all_to_all | solution.py:74
  66.8 4.5 copy-start.5
  73.8 16.8 %copy-start.9 = (bf16[2048]{0:T(1024)(128)(2,1)S(1)}, bf16[2048]{0:T(1024)(128)(2,1)}, u32[]{:S(2)}) copy-start(bf16[2048]{0:T(1024)(128)(2,1)} %param.18) | copy-start | bytes 12292
  86.4 17.2 %all-to-all-start.1 = ((bf16[4,2,32768]{2,1,0:T(2,128)(2,1)}), bf16[4,2,32768]{2,1,0:T(2,128)(2,1)}, u32[]{:S(2)}, u32[]{:S(2)}) async-start(bf16[4,2,32768]{2,1,0:T(2,128)(2,1)} %reshape.278), calls=%async_computation.1 | async-start | bytes 1048576 | tf_op jit(solution)/shard_map/all_to_all | solution.py:95
  103.6 33.8 %all-to-all-start.2 = ((bf16[16,1,80]{2,1,0:T(2,128)(2,1)}), bf16[16,1,80]{2,1,0:T(2,128)(2,1)S(1)}, u32[]{:S(2)}, u32[]{:S(2)}) async-start(bf16[16,1,80]{2,1,0:T(2,128)(2,1)} %all_to_all.47), calls=%async_computation.2 | async-start | bytes 16384 | tf_op jit(solution)/shard_map/all_to_all | solution.py:128
  123.4 1.0 copy-start.2
  137.4 122.9 %all-to-all-start.3 = ((bf16[16,80,2048]{2,1,0:T(8,128)(2,1)}), bf16[16,80,2048]{2,1,0:T(8,128)(2,1)}, u32[]{:S(2)}, u32[]{:S(2)}) async-start(bf16[16,80,2048]{2,1,0:T(8,128)(2,1)} %bitcast.122), calls=%async_computation.3 | async-start | bytes 10485760 | tf_op jit(solution)/shard_map/all_to_all | solution.py:127
  280.0 7.3 %copy-start.4 = (bf16[1280,2048]{1,0:T(8,128)(2,1)S(1)}, bf16[1280,2048]{1,0:T(8,128)(2,1)}, u32[]{:S(2)}) copy-start(bf16[1280,2048]{1,0:T(8,128)(2,1)} %gather_fusion.3) | copy-start | bytes 15728644
  280.0 7.3 %copy-start.11 = (bf16[1,2048,768]{2,1,0:T(8,128)(2,1)S(1)}, bf16[1,2048,768]{2,1,0:T(8,128)(2,1)}, u32[]{:S(2)}) copy-start(bf16[1,2048,768]{2,1,0:T(8,128)(2,1)} %param.22) | copy-start | bytes 9437188
  328.8 121.3 %all-to-all-start.4 = ((bf16[16,80,2048]{2,1,0:T(8,128)(2,1)}), bf16[16,80,2048]{2,1,0:T(8,128)(2,1)}, u32[]{:S(2)}, u32[]{:S(2)}) async-start(bf16[16,80,2048]{2,1,0:T(8,128)(2,1)} %bitcast.123), calls=%async_computation.4 | async-start | bytes 10485760 | tf_op jit(solution)/shard_map/all_to_all | solution.py:167
  450.2 18.3 %copy-start.1 = (bf16[1,768,2048]{2,1,0:T(8,128)(2,1)S(1)}, bf16[1,768,2048]{2,1,0:T(8,128)(2,1)}, u32[]{:S(2)}) copy-start(bf16[1,768,2048]{2,1,0:T(8,128)(2,1)} %param.23) | copy-start | bytes 9437188
  462.4 5.1 %copy-start.3 = (f32[128,2048]{1,0:T(8,128)S(1)}, f32[128,2048]{1,0:T(8,128)}, u32[]{:S(2)}) copy-start(f32[128,2048]{1,0:T(8,128)} %copy-done.2) | copy-start | bytes 3145732
Sparse Core Ops, SparseCore 0:
  8.9 69.4 all-gather.1
where the time goes:
time: 482 us; the launch traced here: 476 us
  waiting for transfers between devices  218 us (45%)
  local copies, waits for them, and re-layouts  123 us (26%)
  other arithmetic  35.1 us (7%)
  matrix products  30.5 us (6%)
  blocking collectives  26.9 us (6%)
  starting transfers between devices  26.3 us (5%)
  between operations  14.7 us (3%)
    all_to_all x1, waiting for transfers between devices, per_device(): lax.all_to_all(returned, ('seq', 'sub'), split_axis=0, concat_axis=0, til...  117 us
    all_to_all x1, waiting for transfers between devices, per_device(): lax.all_to_all(send_rows, ('seq', 'sub'), split_axis=0, concat_axis=0, ti...  101 us
    unnamed x34, local copies, waits for them, and re-layouts  21 us
    unnamed x2, other arithmetic  18.9 us
    all_gather x1, blocking collectives, per_device(): lax.all_gather(key_rows, 'seq', axis=1, tiled=True)  18.7 us
    gather x1, local copies, waits for them, and re-layouts, per_device(): jnp.concatenate([recv_rows.reshape(slots_in, D), jnp.zeros((1, D), jnp.bf...  14 us
    gather x1, local copies, waits for them, and re-layouts, per_device(): jnp.concatenate([results, jnp.zeros((1, D), jnp.bfloat16)], axis=0)[dest]  14 us
    gather x1, local copies, waits for them, and re-layouts, per_device(): gathered = back[slot_of].reshape(tokens, topk, D).astype(jnp.float32)  12.2 us
  transfers between devices with their start and end apart: 6, of which 2 were waited for; matrix products, arithmetic and copies ran while one was open for 21% of the time, Pallas kernels for 0%

commit v1 on v0

--- a/solution.py
+++ b/solution.py
@@ -1,6 +1,9 @@
+import functools
 import jax
 import jax.numpy as jnp
 from jax import lax
+from jax.experimental import pallas as pl
+from jax.experimental.pallas import tpu as pltpu
 from jax.sharding import PartitionSpec as P
 
 D = 2048
@@ -53,7 +56,7 @@
     return ranks.reshape(items).astype(jnp.int32)
 
 
-def per_device(
+def per_device_routed(
     query_rows,
     key_rows,
     value_rows,
@@ -172,6 +175,144 @@
     return (wide + mixture).astype(jnp.bfloat16)[None]
 
 
+def attend_project_kernel(heads, q_ref, k_ref, v_ref, w_ref, o_ref):
+    block = q_ref.shape[0]
+    length = k_ref.shape[0]
+    start = pl.program_id(0) * block
+    row_pos = start + lax.broadcasted_iota(jnp.int32, (block, length), 0)
+    col_pos = lax.broadcasted_iota(jnp.int32, (block, length), 1)
+    allowed = row_pos >= col_pos
+    scale = 1.0 / HD**0.5
+    outs = []
+    for head in range(heads):
+        q = q_ref[:, head * HD : (head + 1) * HD]
+        scores = (
+            lax.dot_general(
+                q, k_ref[...], (((1,), (1,)), ((), ())), preferred_element_type=jnp.float32
+            )
+            * scale
+        )
+        scores = jnp.where(allowed, scores, -1e30)
+        weights = jnp.exp(scores - jnp.max(scores, axis=1, keepdims=True))
+        total = jnp.sum(weights, axis=1, keepdims=True)
+        probs = (weights * (1.0 / total)).astype(jnp.bfloat16)
+        outs.append(
+            jnp.dot(probs, v_ref[...], preferred_element_type=jnp.float32).astype(jnp.bfloat16)
+        )
+    attended = jnp.concatenate(outs, axis=1)
+    o_ref[...] = jnp.dot(attended, w_ref[...], preferred_element_type=jnp.float32).astype(
+        o_ref.dtype
+    )
+
+
+def attend_project(queries, keys, values, weights):
+    length = queries.shape[0]
+    block = min(128, length)
+    width = queries.shape[1]
+    return pl.pallas_call(
+        functools.partial(attend_project_kernel, width // HD),
+        grid=(length // block,),
+        in_specs=[
+            pl.BlockSpec((block, width), lambda i: (i, 0)),
+            pl.BlockSpec((length, HD), lambda i: (0, 0)),
+            pl.BlockSpec((length, HD), lambda i: (0, 0)),
+            pl.BlockSpec(weights.shape, lambda i: (0, 0)),
+        ],
+        out_specs=pl.BlockSpec((block, weights.shape[1]), lambda i: (i, 0)),
+        out_shape=jax.ShapeDtypeStruct((length, weights.shape[1]), jnp.bfloat16),
+        name="attend_project",
+    )(queries, keys, values, weights)
+
+
+def expert_kernel(x_ref, c_ref, wg_ref, wu_ref, wd_ref, o_ref):
+    x = x_ref[...]
+    gate = jnp.dot(x, wg_ref[...], preferred_element_type=jnp.float32)
+    up = jnp.dot(x, wu_ref[...], preferred_element_type=jnp.float32)
+    inner = (gate / (1.0 + jnp.exp(-gate)) * up).astype(jnp.bfloat16)
+    out = jnp.dot(inner, wd_ref[...], preferred_element_type=jnp.float32)
+    o_ref[...] = (out * c_ref[...]).astype(jnp.bfloat16)
+
+
+def expert_rows(rows, coeffs, w_gate, w_up, w_down):
+    count, width = rows.shape
+    block = 256
+    return pl.pallas_call(
+        expert_kernel,
+        grid=(count // block,),
+        in_specs=[
+            pl.BlockSpec((block, width), lambda i: (i, 0)),
+            pl.BlockSpec((block, 1), lambda i: (i, 0)),
+            pl.BlockSpec(w_gate.shape, lambda i: (0, 0), pipeline_mode=pl.Buffered(1)),
+            pl.BlockSpec(w_up.shape, lambda i: (0, 0), pipeline_mode=pl.Buffered(1)),
+            pl.BlockSpec(w_down.shape, lambda i: (0, 0), pipeline_mode=pl.Buffered(1)),
+        ],
+        out_specs=pl.BlockSpec((block, width), lambda i: (i, 0)),
+        out_shape=jax.ShapeDtypeStruct((count, width), jnp.bfloat16),
+        name="expert_rows",
+    )(rows, coeffs, w_gate, w_up, w_down)
+
+
+def per_device_dense(
+    query_rows,
+    key_rows,
+    value_rows,
+    residual_in,
+    out_proj,
+    norm_gain,
+    expert_ids,
+    gate_weights,
+    expert_gate,
+    expert_up,
+    expert_down,
+):
+    n_seq = lax.axis_size("seq")
+    n_sub = lax.axis_size("sub")
+    experts = n_seq * n_sub
+    heads_here = QH // n_seq
+    group = QH // KVH
+    chosen = expert_ids[0][:, :, None] == jnp.arange(experts, dtype=jnp.int32)[None, None, :]
+    coeffs_local = jnp.sum(
+        jnp.where(chosen, gate_weights[0].astype(jnp.float32)[:, :, None], 0.0), axis=1
+    ).astype(jnp.bfloat16)
+    coeffs_all = lax.all_gather(coeffs_local, ("seq", "sub"), axis=0, tiled=True)
+    my_expert = lax.axis_index("seq") * n_sub + lax.axis_index("sub")
+    coeffs = lax.dynamic_slice_in_dim(coeffs_all, my_expert, 1, 1).astype(jnp.float32)
+
+    query_local = lax.all_to_all(query_rows[0], "seq", split_axis=1, concat_axis=0, tiled=True)
+    key_values = lax.all_gather(
+        jnp.concatenate([key_rows[0], value_rows[0]], axis=1), "seq", axis=0, tiled=True
+    )
+    kv_start = lax.axis_index("seq") * heads_here // group * HD
+    keys = lax.dynamic_slice_in_dim(key_values, kv_start, HD, 1)
+    values = lax.dynamic_slice_in_dim(key_values, KVH * HD + kv_start, HD, 1)
+    partial = attend_project(query_local, keys, values, out_proj)
+    projected = lax.psum_scatter(partial, "seq", scatter_dimension=0, tiled=True)
+    hidden = (residual_in[0].astype(jnp.float32) + projected.astype(jnp.float32)).astype(
+        jnp.bfloat16
+    )
+    wide = hidden.astype(jnp.float32)
+    normed = (
+        wide
+        * lax.rsqrt(jnp.mean(wide * wide, axis=1, keepdims=True) + 1e-06)
+        * norm_gain.astype(jnp.float32)
+    ).astype(jnp.bfloat16)
+    rows = lax.all_gather(normed, ("seq", "sub"), axis=0, tiled=True)
+    results = expert_rows(rows, coeffs, expert_gate[0], expert_up[0], expert_down[0])
+    mixture = lax.psum_scatter(results, ("seq", "sub"), scatter_dimension=0, tiled=True)
+    return (wide + mixture.astype(jnp.float32)).astype(jnp.bfloat16)[None]
+
+
+def per_device(*args):
+    tokens = args[0].shape[1]
+    topk = args[6].shape[2]
+    n_seq = lax.axis_size("seq")
+    experts = n_seq * lax.axis_size("sub")
+    cap = max(2, (5 * tokens * topk + 4 * experts - 1) // (4 * experts))
+    if 2 * cap >= tokens and QH // n_seq <= QH // KVH:
+        return per_device_dense(*args)
+    return per_device_routed(*args)
+
+
 def solution(mesh):
     placed = (
         P(("grp", "sub"), "seq", None),

time: 482 us -> 291 us (0.60); the launches traced: 476 us -> 290 us
  local copies, waits for them, and re-layouts: 123 us -> 4.03 us
  waiting for transfers between devices: 218 us -> 171 us
  Pallas kernels: 0 us -> 36.5 us
  matrix products: 30.5 us -> 0 us
  other arithmetic: 35.1 us -> 6.64 us
  blocking collectives: 26.9 us -> 54.8 us
  starting transfers between devices: 26.3 us -> 4.35 us
    all_to_all x5 -> x1, waiting for transfers between devices: 218 us -> 0.01 us  [per_device_dense(): lax.all_to_all(query_rows[0], 'seq', split_axis=1, concat_axis=0, tiled=T...]
    reduce_scatter x0 -> x2, waiting for transfers between devices: none -> 134 us  [the longest x1 102 us: per_device_dense(): lax.psum_scatter(results, ('seq', 'sub'), scatter_dimension=0, tiled=True)]
    gather x6 -> x0, local copies, waits for them, and re-layouts: 68.1 us -> none  [the longest x1 14 us: per_device(): jnp.concatenate([recv_rows.reshape(slots_in, D), jnp.zeros((1, D), jnp.bf...]
    pallas_call x0 -> x2, Pallas kernels: none -> 36.5 us  [the longest x1 26.2 us: expert_rows(): pl.pallas_call(expert_kernel, grid=(count // block,), in_specs=[pl.BlockS...]
    all_gather x1, waiting for transfers between devices: 0.01 us -> 36.3 us  [per_device_dense(): rows = lax.all_gather(normed, ('seq', 'sub'), axis=0, tiled=True)]
    dot_general x13 -> x0, matrix products: 30.5 us -> none  [the longest x1 7.24 us: expert_block(): jnp.dot(compact_rows, w_gate, preferred_element_type=jnp.float32)]
    all_gather x2, blocking collectives: 26.9 us -> 54.8 us  [the longest x1 42.3 us: per_device_dense(): lax.all_gather(coeffs_local, ('seq', 'sub'), axis=0, tiled=True)]
    all_to_all x5 -> x1, starting transfers between devices: 26.3 us -> 4.26 us  [per_device_dense(): lax.all_to_all(query_rows[0], 'seq', split_axis=1, concat_axis=0, tiled=T...]
  transfers between devices with their start and end apart: 6 -> 4, of which waited for: 2 -> 3; matrix products, arithmetic and copies ran while one was open for 21% -> 1% of each run, Pallas kernels for 0% -> 0%
where the time goes in v1:
time: 291 us; the launch traced here: 290 us
  waiting for transfers between devices  171 us (59%)
  blocking collectives  54.8 us (19%)
  Pallas kernels  36.5 us (13%)
  between operations  13.2 us (5%)
  other arithmetic  6.64 us (2%)
  starting transfers between devices  4.35 us (1%)
  local copies, waits for them, and re-layouts  4.03 us (1%)
    reduce_scatter x1, waiting for transfers between devices, per_device_dense(): lax.psum_scatter(results, ('seq', 'sub'), scatter_dimension=0, tiled=True)  102 us
    all_gather x1, blocking collectives, per_device_dense(): lax.all_gather(coeffs_local, ('seq', 'sub'), axis=0, tiled=True)  42.3 us
    all_gather x1, waiting for transfers between devices, per_device_dense(): rows = lax.all_gather(normed, ('seq', 'sub'), axis=0, tiled=True)  36.3 us
    reduce_scatter x1, waiting for transfers between devices, per_device_dense(): lax.psum_scatter(partial, 'seq', scatter_dimension=0, tiled=True)  32.2 us
    pallas_call x1, Pallas kernels, expert_rows(): pl.pallas_call(expert_kernel, grid=(count // block,), in_specs=[pl.BlockS...  26.2 us
    all_gather x1, blocking collectives, per_device_dense(): lax.all_gather(jnp.concatenate([key_rows[0], value_rows[0]], axis=1), 'se...  12.5 us
    pallas_call x1, Pallas kernels, attend_project(): pl.pallas_call(functools.partial(attend_project_kernel, width // HD), gri...  10.3 us
  transfers between devices with their start and end apart: 4, of which 3 were waited for; matrix products, arithmetic and copies ran while one was open for 1% of the time, Pallas kernels for 0%

profile of v1, /device:TPU:0, one launch (start us, length us, event | category | flops | bytes accessed | tf_op | source)
XLA Modules:
  0.0 290.2 jit_solution(17453310173921350733)
XLA Ops:
  6.5 0.0 copy-start.3
  6.5 0.0 copy-start.4
  6.5 1.5 all_to_all.14
  8.0 0.9 copy.17
  8.9 4.3 %all-to-all-start = ((bf16[128,4,512]{2,0,1:T(8,128)(2,1)}), bf16[128,4,512]{2,0,1:T(8,128)(2,1)S(1)}, u32[]{:S(2)}, u32[]{:S(2)}) async-start(bf16[128,4,512]{2,0,1:T(8,128)(2,1)} %copy.17), calls=%async_computation | async-start | bytes 1048576 | tf_op jit(solution)/shard_map/all_to_all | solution.py:281
  13.2 0.0 reduce-scatter.3.cloned.1.call-start
  13.2 0.0 copy-done.3
  13.2 0.0 copy-done.4
  13.2 12.5 %all_gather.9 = bf16[512,512]{1,0:T(8,128)(2,1)S(1)} all-gather(bf16[128,512]{1,0:T(8,128)(2,1)S(1)} %pad_maximum_fusion), channel_id=1, replica_groups=mesh['grp'=2,'seq'=4,'sub'=4] {'seq'}, dimensions={0}, use_global_device_ids=true | all-gather | bytes 655360 | tf_op jit(solution)/shard_map/all_gather | solution.py:282
  25.6 0.7 constant_dynamic-slice_fusion
  26.4 0.0 all-to-all-done
  26.4 0.0 copy-start.2
  26.4 0.8 copy-done.2
  27.2 0.0 copy-start.5
  27.2 0.0 copy-start
  27.2 10.3 %attend_project.1 = bf16[512,2048]{1,0:T(8,128)(2,1)} custom-call(bf16[512,512]{1,0:T(8,128)(2,1)} %bitcast.26, bf16[512,128]{1,0:T(8,128)(2,1)} %get-tuple-element.6.k_ref, bf16[512,128]{1,0:T(8,128)(2,1)} %get-tuple-element.5.v_ref, bf16[512,2048]{1,0:T(8,128)(2,1)} %w_ref.1), custom_call_target="tpu_custom_call" | custom-call | tf_op jit(solution)/shard_map/attend_project/pallas_call | solution.py:212
  37.5 0.0 copy-start.7
  37.5 0.0 copy-start.6
  37.5 0.0 reduce-scatter.3.cloned.1.call-update
  37.5 0.0 all-gather.2.cloned.1.call-start
  37.5 0.0 copy-done.5
  37.6 32.2 %reduce-scatter.3.cloned.1.call-done = bf16[128,2048]{1,0:T(8,128)(2,1)} async-done(((bf16[512,2048]{1,0:T(8,128)(2,1)}), bf16[128,2048]{1,0:T(8,128)(2,1)}) %reduce-scatter.3.cloned.1.call-update) | async-done | bytes 524304 | tf_op jit(solution)/shard_map/reduce_scatter | solution.py:289
  69.8 0.0 copy-done
  69.8 1.3 fusion
  71.1 2.0 fusion.2
  73.1 0.0 all-gather.2.cloned.1.call-update
  73.1 0.0 reduce-scatter.5.cloned.1.call-start
  73.2 0.0 copy-done.7
  73.2 0.0 copy-done.6
  73.3 0.1 copy.18
  73.4 42.3 %all_gather.11 = bf16[2048,16]{1,0:T(8,128)(2,1)S(1)} all-gather(bf16[128,16]{1,0:T(8,128)(2,1)S(1)} %copy.18), channel_id=1, replica_groups=mesh['grp'=2,'seq'=4,'sub'=4] {'seq','sub'}, dimensions={0}, use_global_device_ids=true | all-gather | bytes 69632 | tf_op jit(solution)/shard_map/all_gather | solution.py:277
  115.7 1.2 dynamic-slice_convert_fusion.c_ref
  116.9 36.3 %all-gather.2.cloned.1.call-done.x_ref = bf16[2048,2048]{1,0:T(8,128)(2,1)} async-done(((bf16[128,2048]{1,0:T(8,128)(2,1)}), bf16[2048,2048]{1,0:T(8,128)(2,1)}) %all-gather.2.cloned.1.call-update) | async-done | bytes 8388624 | tf_op jit(solution)/shard_map/all_gather | solution.py:299
  153.2 26.2 %expert_rows.1 = bf16[2048,2048]{1,0:T(8,128)(2,1)} custom-call(bf16[2048,2048]{1,0:T(8,128)(2,1)} %all-gather.2.cloned.1.call-done.x_ref, f32[2048,1]{1,0:T(8,128)} %dynamic-slice_convert_fusion.c_ref, bf16[2048,768]{1,0:T(8,128)(2,1)} %bitcast.23, bf16[2048,768]{1,0:T(8,128)(2,1)} %bitcast.24, bf16[768,2048]{1,0:T(8,128)(2,1)} %bitcast.25), custom_call_target="tpu_custom_call" | custom-call | tf_op jit(solution)/shard_map/expert_rows/pallas_call | solution.py:239
  179.4 0.0 copy-start.1
  179.4 0.0 reduce-scatter.5.cloned.1.call-update
  179.4 102.1 %reduce-scatter.5.cloned.1.call-done = bf16[128,2048]{1,0:T(8,128)(2,1)} async-done(((bf16[2048,2048]{1,0:T(8,128)(2,1)}), bf16[128,2048]{1,0:T(8,128)(2,1)}) %reduce-scatter.5.cloned.1.call-update) | async-done | bytes 524304 | tf_op jit(solution)/shard_map/reduce_scatter | solution.py:301
  281.6 0.0 copy-done.1
  281.6 2.1 fusion.5
  (5 shorter events, 0.0 us)
Async XLA Ops:
  6.5 6.6 %copy-start.3 = (bf16[1,128,256]{2,1,0:T(8,128)(2,1)S(1)}, bf16[1,128,256]{2,1,0:T(8,128)(2,1)}, u32[]{:S(2)}) copy-start(bf16[1,128,256]{2,1,0:T(8,128)(2,1)} %param.13) | copy-start | bytes 196612
  6.5 6.6 %copy-start.4 = (bf16[1,128,256]{2,1,0:T(8,128)(2,1)S(1)}, bf16[1,128,256]{2,1,0:T(8,128)(2,1)}, u32[]{:S(2)}) copy-start(bf16[1,128,256]{2,1,0:T(8,128)(2,1)} %param.12) | copy-start | bytes 196612
  8.9 17.5 %all-to-all-start = ((bf16[128,4,512]{2,0,1:T(8,128)(2,1)}), bf16[128,4,512]{2,0,1:T(8,128)(2,1)S(1)}, u32[]{:S(2)}, u32[]{:S(2)}) async-start(bf16[128,4,512]{2,0,1:T(8,128)(2,1)} %copy.17), calls=%async_computation | async-start | bytes 1048576 | tf_op jit(solution)/shard_map/all_to_all | solution.py:281
  13.2 56.6 %reduce-scatter.3.cloned.1.call-start = ((), (), s32[]{:S(2)}) async-start(), calls=%async_computation.3 | async-start | bytes 2621440 | tf_op jit(solution)/shard_map/reduce_scatter | solution.py:289
  26.4 0.8 copy-start.2
  27.2 10.4 %copy-start.5 = (bf16[2048]{0:T(1024)(128)(2,1)S(1)}, bf16[2048]{0:T(1024)(128)(2,1)}, u32[]{:S(2)}) copy-start(bf16[2048]{0:T(1024)(128)(2,1)} %param.16) | copy-start | bytes 12292
  27.2 42.6 %copy-start = (bf16[1,128,2048]{2,1,0:T(8,128)(2,1)S(1)}, bf16[1,128,2048]{2,1,0:T(8,128)(2,1)}, u32[]{:S(2)}) copy-start(bf16[1,128,2048]{2,1,0:T(8,128)(2,1)} %param.14) | copy-start | bytes 1572868
  37.5 35.7 %copy-start.7 = (bf16[1,128,8]{1,2,0:T(8,128)(2,1)S(1)}, bf16[1,128,8]{1,2,0:T(8,128)(2,1)}, u32[]{:S(2)}) copy-start(bf16[1,128,8]{1,2,0:T(8,128)(2,1)} %param.18) | copy-start | bytes 6148
  37.5 35.8 %copy-start.6 = (s32[1,128,8]{1,2,0:T(8,128)S(1)}, s32[1,128,8]{1,2,0:T(8,128)}, u32[]{:S(2)}) copy-start(s32[1,128,8]{1,2,0:T(8,128)} %param.17) | copy-start | bytes 12292
  37.5 115.7 %all-gather.2.cloned.1.call-start = ((), (), s32[]{:S(2)}) async-start(), calls=%async_computation.4 | async-start | bytes 8912896 | tf_op jit(solution)/shard_map/all_gather | solution.py:299
  73.1 208.4 %reduce-scatter.5.cloned.1.call-start = ((), (), s32[]{:S(2)}) async-start(), calls=%async_computation.5 | async-start | bytes 8912896 | tf_op jit(solution)/shard_map/reduce_scatter | solution.py:301
  179.4 102.2 %copy-start.1 = (bf16[128,2048]{1,0:T(8,128)(2,1)S(1)}, bf16[128,2048]{1,0:T(8,128)(2,1)}, u32[]{:S(2)}) copy-start(bf16[128,2048]{1,0:T(8,128)(2,1)} %reduce-scatter.3.cloned.1.call-done) | copy-start | bytes 1572868
Sparse Core Ops, SparseCore 0:
  37.6 32.1 reduce-scatter.2
  73.3 79.8 all-gather.1
  179.6 101.9 reduce-scatter.4

commit v2 on v1

--- a/solution.py
+++ b/solution.py
@@ -224,32 +224,380 @@
     )(queries, keys, values, weights)
 
 
-def expert_kernel(x_ref, c_ref, wg_ref, wu_ref, wd_ref, o_ref):
-    x = x_ref[...]
-    gate = jnp.dot(x, wg_ref[...], preferred_element_type=jnp.float32)
-    up = jnp.dot(x, wu_ref[...], preferred_element_type=jnp.float32)
-    inner = (gate / (1.0 + jnp.exp(-gate)) * up).astype(jnp.bfloat16)
-    out = jnp.dot(inner, wd_ref[...], preferred_element_type=jnp.float32)
-    o_ref[...] = (out * c_ref[...]).astype(jnp.bfloat16)
-
-
-def expert_rows(rows, coeffs, w_gate, w_up, w_down):
-    count, width = rows.shape
-    block = 256
+def nearest_order(n):
+    return [sorted(range(n), key=lambda p: (abs(p - z), p)) for z in range(n)]
+
+
+def lookup(table, i, j):
+    total = 0
+    for a, row in enumerate(table):
+        for b, value in enumerate(row):
+            if value:
+                hit = jnp.logical_and(i == a, j == b)
+                total = total + jnp.where(hit, value, 0)
+    return total
+
+
+def experts_kernel(
+    n_sub,
+    x_hbm,
+    wide_ref,
+    wg_hbm,
+    wu_hbm,
+    wd_hbm,
+    o_ref,
+    rows,
+    outs,
+    from_core,
+    from_y,
+    from_low,
+    from_high,
+    wg,
+    wu,
+    wd,
+    load_sem,
+    row_recv,
+    up_send,
+    down_send,
+    y_send,
+    core_send,
+    relay_send,
+    core_recv,
+    result_send,
+    y_recv,
+    result_y_send,
+    low_recv,
+    high_recv,
+    result_up_send,
+    result_down_send,
+):
+    seq = lax.axis_index("seq")
+    z = lax.axis_index("sub")
+    y = seq // 2
+    c = seq % 2
+    tokens = wide_ref.shape[0]
+    width = wide_ref.shape[1]
+    half = tokens // 2
+    order = nearest_order(n_sub)
+    me = seq * n_sub + z
+    high = {"sub": z + 1}
+    low = {"sub": z - 1}
+    across = {"seq": (1 - y) * 2 + c}
+    partner = {"seq": y * 2 + 1 - c}
+    has_high = z < n_sub - 1
+    has_low = z > 0
+
+    def slot(yy, p, cc):
+        return (yy * n_sub + p) * 2 + cc
+
+    def piece(ref, index, h):
+        return ref.at[pl.ds(pl.multiple_of(index * tokens + h * half, half), half), :]
+
+    def remote(src, dst, send, recv, target):
+        return pltpu.make_async_remote_copy(
+            src_ref=src,
+            dst_ref=dst,
+            send_sem=send,
+            recv_sem=recv,
+            device_id=target,
+            device_id_type=pl.DeviceIdType.MESH,
+        )
+
+    loads = [
+        pltpu.make_async_copy(x_hbm, rows.at[pl.ds(pl.multiple_of(slot(y, z, c) * tokens, tokens), tokens), :], load_sem.at[0]),
+        pltpu.make_async_copy(wg_hbm, wg, load_sem.at[1]),
+        pltpu.make_async_copy(wu_hbm, wu, load_sem.at[2]),
+        pltpu.make_async_copy(wd_hbm, wd, load_sem.at[3]),
+    ]
+    for load in loads:
+        load.start()
+
+    barrier = pltpu.get_barrier_semaphore()
+    pl.semaphore_signal(barrier, 1, device_id=across, device_id_type=pl.DeviceIdType.MESH)
+    pl.semaphore_signal(barrier, 1, device_id=partner, device_id_type=pl.DeviceIdType.MESH)
+
+    @pl.when(has_high)
+    def _():
+        pl.semaphore_signal(barrier, 1, device_id=high, device_id_type=pl.DeviceIdType.MESH)
+
+    @pl.when(has_low)
+    def _():
+        pl.semaphore_signal(barrier, 1, device_id=low, device_id_type=pl.DeviceIdType.MESH)
+
+    peers = 2 + jnp.where(has_high, 1, 0) + jnp.where(has_low, 1, 0)
+    pl.semaphore_wait(barrier, peers)
+
+    loads[0].wait()
+
+    def row_copy(index, h, send, target):
+        here = piece(rows, index, h)
+        return remote(here, here, send, row_recv.at[index * 2 + h], target)
+
+    def wait_rows(index, h):
+        row_copy(index, h, relay_send.at[0], partner).wait_recv()
+
+    def column_copies(p, h):
+        index = slot(y, p, c)
+        at = p * 2 + h
+        return (
+            (jnp.logical_and(p <= z, has_high), row_copy(index, h, up_send.at[at], high)),
+            (jnp.logical_and(p >= z, has_low), row_copy(index, h, down_send.at[at], low)),
+            (None, row_copy(index, h, y_send.at[at], across)),
+            (None, row_copy(index, h, core_send.at[at], partner)),
+        )
+
+    def spread(p, h):
+        for condition, copy in column_copies(p, h):
+            if condition is None:
+                copy.start()
+            else:
+
+                @pl.when(condition)
+                def _():
+                    copy.start()
+
+    def relay_copy(p, h):
+        return row_copy(slot(1 - y, p, c), h, relay_send.at[p * 2 + h], partner)
+
+    def result_copy(yy, p):
+        index = slot(yy, p, 1 - c)
+        pair = yy * n_sub + p
+        src = outs.at[pl.ds(pl.multiple_of(index * tokens, tokens), tokens), :]
+        dst = from_core.at[pl.ds(pl.multiple_of(pair * tokens, tokens), tokens), :]
+        return remote(src, dst, result_send.at[pair], core_recv.at[pair], partner)
+
+    def compute(yy, p):
+        wait_rows(slot(yy, p, 1 - c), 0)
+        wait_rows(slot(yy, p, 1 - c), 1)
+        at = pl.ds(pl.multiple_of((yy * n_sub + p) * 2 * tokens, 2 * tokens), 2 * tokens)
+        x = rows[at, :width]
+        gains = rows[at, width:].astype(jnp.float32)
+        lane = lax.broadcasted_iota(jnp.int32, gains.shape, 1)
+        coeff = jnp.sum(jnp.where(lane == me, gains, 0.0), axis=1, keepdims=True)
+        gate = jnp.dot(x, wg[...], preferred_element_type=jnp.float32)
+        up = jnp.dot(x, wu[...], preferred_element_type=jnp.float32)
+        inner = (gate / (1.0 + jnp.exp(-gate)) * up).astype(jnp.bfloat16)
+        out = jnp.dot(inner, wd[...], preferred_element_type=jnp.float32)
+        outs[at, :] = (out * coeff).astype(jnp.bfloat16)
+        result_copy(yy, p).start()
+
+    def gather_step(k, carry):
+        t = k // 2
+        other = k % 2
+
+        @pl.when(other == 0)
+        def _():
+            p = lookup(order, z, t)
+
+            @pl.when(t > 0)
+            def _():
+                wait_rows(slot(y, p, c), 0)
+
+            spread(p, 0)
+
+            @pl.when(t > 0)
+            def _():
+                wait_rows(slot(y, p, c), 1)
+
+            spread(p, 1)
+
+        @pl.when(k == 0)
+        def _():
+            for load in loads[1:]:
+                load.wait()
+
+        p = lookup(order, z, t)
+
+        @pl.when(other == 1)
+        def _():
+            wait_rows(slot(1 - y, p, c), 0)
+            relay_copy(p, 0).start()
+            wait_rows(slot(1 - y, p, c), 1)
+            relay_copy(p, 1).start()
+
+        compute(jnp.where(other == 1, 1 - y, y), p)
+        return carry
+
+    lax.fori_loop(0, 2 * n_sub, gather_step, 0)
+
+    def wide_load(ref, index, h):
+        at = pl.ds(pl.multiple_of(index * tokens + h * half, half), half)
+        return ref[at, :].astype(jnp.float32)
+
+    def y_copy(p, h):
+        at = p * 2 + h
+        return remote(
+            piece(outs, slot(1 - y, p, c), h),
+            piece(from_y, p, h),
+            result_y_send.at[at],
+            y_recv.at[at],
+            across,
+        )
+
+    def z_copy(p, h, buffer, send, recv, target):
+        at = p * 2 + h
+        return remote(
+            piece(outs, slot(y, p, c), h), piece(buffer, p, h), send.at[at], recv.at[at], target
+        )
+
+    def up_copy(p, h):
+        return z_copy(p, h, from_low, result_up_send, low_recv, high)
+
+    def down_copy(p, h):
+        return z_copy(p, h, from_high, result_down_send, high_recv, low)
+
+    def store_out(index, h, value):
+        at = pl.ds(pl.multiple_of(index * tokens + h * half, half), half)
+        outs[at, :] = value.astype(jnp.bfloat16)
+
+    def y_step(k, carry):
+        p = lookup(order, z, n_sub - 1 - k)
+        result_copy(1 - y, p).wait_recv()
+        index = slot(1 - y, p, c)
+        for h in range(2):
+            store_out(
+                index, h, wide_load(outs, index, h) + wide_load(from_core, (1 - y) * n_sub + p, h)
+            )
+            y_copy(p, h).start()
+        return carry
+
+    lax.fori_loop(0, n_sub, y_step, 0)
+
+    def own_step(k, carry):
+        p = lookup(order, z, n_sub - 1 - k)
+        result_copy(y, p).wait_recv()
+        index = slot(y, p, c)
+        store = wide_load(outs, index, 0) + wide_load(from_core, y * n_sub + p, 0)
+        store_out(index, 0, store)
+        store = wide_load(outs, index, 1) + wide_load(from_core, y * n_sub + p, 1)
+        store_out(index, 1, store)
+        return carry
+
+    lax.fori_loop(0, n_sub, own_step, 0)
+
+    def z_step(k, carry):
+        p = lookup(order, z, n_sub - 1 - k // 2)
+        h = k % 2
+        index = slot(y, p, c)
+        y_copy(p, h).wait_recv()
+
+        @pl.when(p > z)
+        def _():
+            store_out(index, h, wide_load(outs, index, h) + wide_load(from_y, p, h))
+
+            @pl.when(has_low)
+            def _():
+                up_copy(p, h).wait_recv()
+                store_out(index, h, wide_load(outs, index, h) + wide_load(from_low, p, h))
+
+            up_copy(p, h).start()
+
+        @pl.when(p < z)
+        def _():
+            store_out(index, h, wide_load(outs, index, h) + wide_load(from_y, p, h))
+
+            @pl.when(has_high)
+            def _():
+                down_copy(p, h).wait_recv()
+                store_out(index, h, wide_load(outs, index, h) + wide_load(from_high, p, h))
+
+            down_copy(p, h).start()
+
+        @pl.when(p == z)
+        def _():
+            at = pl.ds(pl.multiple_of(h * half, half), half)
+            store_out(index, h, wide_load(outs, index, h) + wide_load(from_y, p, h))
+
+            @pl.when(has_low)
+            def _():
+                up_copy(p, h).wait_recv()
+                store_out(index, h, wide_load(outs, index, h) + wide_load(from_low, p, h))
+
+            @pl.when(has_high)
+            def _():
+                down_copy(p, h).wait_recv()
+                store_out(index, h, wide_load(outs, index, h) + wide_load(from_high, p, h))
+
+            o_ref[at, :] = (wide_ref[at, :].astype(jnp.float32) + wide_load(outs, index, h)).astype(
+                jnp.bfloat16
+            )
+
+        return carry
+
+    lax.fori_loop(0, 2 * n_sub, z_step, 0)
+
+    def drain(k, carry):
+        p = k // 2
+        h = k % 2
+        for condition, copy in column_copies(p, h):
+            if condition is None:
+                copy.wait_send()
+            else:
+
+                @pl.when(condition)
+                def _():
+                    copy.wait_send()
+
+        relay_copy(p, h).wait_send()
+        y_copy(p, h).wait_send()
+        result_copy(h, p).wait_send()
+
+        @pl.when(p > z)
+        def _():
+            up_copy(p, h).wait_send()
+
+        @pl.when(p < z)
+        def _():
+            down_copy(p, h).wait_send()
+
+        return carry
+
+    lax.fori_loop(0, 2 * n_sub, drain, 0)
+
+
+def experts_exchange(rows_ext, hidden, w_gate, w_up, w_down, n_sub):
+    tokens, width = hidden.shape
+    blocks = 4 * n_sub
+    dma = lambda count: pltpu.SemaphoreType.DMA((count,))
+    any_spec = pl.BlockSpec(memory_space=pl.ANY)
+    vmem_spec = pl.BlockSpec(memory_space=pltpu.VMEM)
+    bf = jnp.bfloat16
     return pl.pallas_call(
-        expert_kernel,
-        grid=(count // block,),
-        in_specs=[
-            pl.BlockSpec((block, width), lambda i: (i, 0)),
-            pl.BlockSpec((block, 1), lambda i: (i, 0)),
-            pl.BlockSpec(w_gate.shape, lambda i: (0, 0), pipeline_mode=pl.Buffered(1)),
-            pl.BlockSpec(w_up.shape, lambda i: (0, 0), pipeline_mode=pl.Buffered(1)),
-            pl.BlockSpec(w_down.shape, lambda i: (0, 0), pipeline_mode=pl.Buffered(1)),
+        functools.partial(experts_kernel, n_sub),
+        in_specs=[any_spec, vmem_spec, any_spec, any_spec, any_spec],
+        out_specs=vmem_spec,
+        out_shape=jax.ShapeDtypeStruct((tokens, width), bf),
+        scratch_shapes=[
+            pltpu.VMEM((blocks * tokens, rows_ext.shape[1]), bf),
+            pltpu.VMEM((blocks * tokens, width), bf),
+            pltpu.VMEM((2 * n_sub * tokens, width), bf),
+            pltpu.VMEM((n_sub * tokens, width), bf),
+            pltpu.VMEM((n_sub * tokens, width), bf),
+            pltpu.VMEM((n_sub * tokens, width), bf),
+            pltpu.VMEM(w_gate.shape, bf),
+            pltpu.VMEM(w_up.shape, bf),
+            pltpu.VMEM(w_down.shape, bf),
+            dma(4),
+            dma(2 * blocks),
+            dma(2 * n_sub),
+            dma(2 * n_sub),
+            dma(2 * n_sub),
+            dma(2 * n_sub),
+            dma(2 * n_sub),
+            dma(2 * n_sub),
+            dma(2 * n_sub),
+            dma(2 * n_sub),
+            dma(2 * n_sub),
+            dma(2 * n_sub),
+            dma(2 * n_sub),
+            dma(2 * n_sub),
+            dma(2 * n_sub),
         ],
-        out_specs=pl.BlockSpec((block, width), lambda i: (i, 0)),
-        out_shape=jax.ShapeDtypeStruct((count, width), jnp.bfloat16),
-        name="expert_rows",
-    )(rows, coeffs, w_gate, w_up, w_down)
+        compiler_params=pltpu.CompilerParams(
+            collective_id=0, has_side_effects=True, vmem_limit_bytes=60 * 2**20
+        ),
+        name="experts_exchange",
+    )(rows_ext, hidden, w_gate, w_up, w_down)
 
 
 def per_device_dense(
@@ -274,9 +622,6 @@
     coeffs_local = jnp.sum(
         jnp.where(chosen, gate_weights[0].astype(jnp.float32)[:, :, None], 0.0), axis=1
     ).astype(jnp.bfloat16)
-    coeffs_all = lax.all_gather(coeffs_local, ("seq", "sub"), axis=0, tiled=True)
-    my_expert = lax.axis_index("seq") * n_sub + lax.axis_index("sub")
-    coeffs = lax.dynamic_slice_in_dim(coeffs_all, my_expert, 1, 1).astype(jnp.float32)
 
     query_local = lax.all_to_all(query_rows[0], "seq", split_axis=1, concat_axis=0, tiled=True)
     key_values = lax.all_gather(
@@ -296,10 +641,13 @@
         * lax.rsqrt(jnp.mean(wide * wide, axis=1, keepdims=True) + 1e-06)
         * norm_gain.astype(jnp.float32)
     ).astype(jnp.bfloat16)
-    rows = lax.all_gather(normed, ("seq", "sub"), axis=0, tiled=True)
-    results = expert_rows(rows, coeffs, expert_gate[0], expert_up[0], expert_down[0])
-    mixture = lax.psum_scatter(results, ("seq", "sub"), scatter_dimension=0, tiled=True)
-    return (wide + mixture.astype(jnp.float32)).astype(jnp.bfloat16)[None]
+    lanes = 128 * ((experts + 127) // 128)
+    rows_ext = jnp.concatenate(
+        [normed, jnp.pad(coeffs_local, ((0, 0), (0, lanes - experts)))], axis=1
+    )
+    return experts_exchange(
+        rows_ext, hidden, expert_gate[0], expert_up[0], expert_down[0], n_sub
+    )[None]
 
 
 def per_device(*args):
@@ -308,7 +656,7 @@
     n_seq = lax.axis_size("seq")
     experts = n_seq * lax.axis_size("sub")
     cap = max(2, (5 * tokens * topk + 4 * experts - 1) // (4 * experts))
-    if 2 * cap >= tokens and QH // n_seq <= QH // KVH:
+    if 2 * cap >= tokens and n_seq == 4:
         return per_device_dense(*args)
     return per_device_routed(*args)
 

time: 291 us -> 212 us (0.73)
  waiting for transfers between devices: 171 us -> 31.5 us
  Pallas kernels: 36.5 us -> 141 us
  blocking collectives: 54.8 us -> 12.5 us
  other arithmetic: 6.64 us -> 2.41 us
    pallas_call x1, Pallas kernels: 26.2 us -> 130 us  [experts_exchange(): pl.pallas_call(functools.partial(experts_kernel, n_sub), in_specs=[any_sp...]
    reduce_scatter x1 -> x0, waiting for transfers between devices: 102 us -> none  [per_device_dense(): lax.psum_scatter(results, ('seq', 'sub'), scatter_dimension=0, tiled=True)]
    all_gather x1 -> x0, blocking collectives: 42.3 us -> none  [per_device_dense(): lax.all_gather(coeffs_local, ('seq', 'sub'), axis=0, tiled=True)]
    all_gather x1 -> x0, waiting for transfers between devices: 36.3 us -> none  [per_device_dense(): rows = lax.all_gather(normed, ('seq', 'sub'), axis=0, tiled=True)]
  transfers between devices with their start and end apart: 4 -> 2, of which waited for: 3 -> 1; matrix products, arithmetic and copies ran while one was open for 1% -> 0% of each run, Pallas kernels for 0% -> 0%
where the time goes in v2:
time: 212 us; the launch traced here: 211 us
  Pallas kernels  141 us (67%)
  waiting for transfers between devices  31.5 us (15%)
  between operations  13.4 us (6%)
  blocking collectives  12.5 us (6%)
  local copies, waits for them, and re-layouts  6.57 us (3%)
  starting transfers between devices  4.27 us (2%)
  other arithmetic  2.41 us (1%)
    pallas_call x1, Pallas kernels, experts_exchange(): pl.pallas_call(functools.partial(experts_kernel, n_sub), in_specs=[any_sp...  130 us
    reduce_scatter x1, waiting for transfers between devices, per_device_dense(): lax.psum_scatter(partial, 'seq', scatter_dimension=0, tiled=True)  31.5 us
    all_gather x1, blocking collectives, per_device_dense(): lax.all_gather(jnp.concatenate([key_rows[0], value_rows[0]], axis=1), 'se...  12.5 us
    pallas_call x1, Pallas kernels, attend_project(): pl.pallas_call(functools.partial(attend_project_kernel, width // HD), gri...  10.2 us
    all_to_all x1, starting transfers between devices, per_device_dense(): lax.all_to_all(query_rows[0], 'seq', split_axis=1, concat_axis=0, tiled=T...  4.26 us
  transfers between devices with their start and end apart: 2, of which 1 were waited for; matrix products, arithmetic and copies ran while one was open for 0% of the time, Pallas kernels for 0%

profile of v2, /device:TPU:0, one launch (start us, length us, event | category | flops | bytes accessed | tf_op | source)
XLA Modules:
  0.0 211.2 jit_solution(16992607758850195034)
XLA Ops:
  6.5 0.0 copy-start.4
  6.5 0.0 copy-start.3
  6.5 1.5 all_to_all.14
  8.0 0.9 copy.17
  8.9 4.3 %all-to-all-start = ((bf16[128,4,512]{2,0,1:T(8,128)(2,1)}), bf16[128,4,512]{2,0,1:T(8,128)(2,1)S(1)}, u32[]{:S(2)}, u32[]{:S(2)}) async-start(bf16[128,4,512]{2,0,1:T(8,128)(2,1)} %copy.17), calls=%async_computation | async-start | bytes 1048576 | tf_op jit(solution)/shard_map/all_to_all | solution.py:626
  13.2 0.0 reduce-scatter.2.cloned.1.call-start
  13.2 0.0 copy-done.4
  13.2 0.0 copy-done.3
  13.2 12.5 %all_gather.3 = bf16[512,512]{1,0:T(8,128)(2,1)S(1)} all-gather(bf16[128,512]{1,0:T(8,128)(2,1)S(1)} %pad_maximum_fusion), channel_id=1, replica_groups=mesh['grp'=2,'seq'=4,'sub'=4] {'seq'}, dimensions={0}, use_global_device_ids=true | all-gather | bytes 655360 | tf_op jit(solution)/shard_map/all_gather | solution.py:627
  25.6 0.7 constant_dynamic-slice_fusion
  26.4 0.0 all-to-all-done
  26.4 0.0 copy-start.1
  26.4 0.8 copy-done.1
  27.2 10.2 %attend_project.1 = bf16[512,2048]{1,0:T(8,128)(2,1)} custom-call(bf16[512,512]{1,0:T(8,128)(2,1)} %bitcast.20, bf16[512,128]{1,0:T(8,128)(2,1)} %get-tuple-element.8.k_ref, bf16[512,128]{1,0:T(8,128)(2,1)} %get-tuple-element.7.v_ref, bf16[512,2048]{1,0:T(8,128)(2,1)} %w_ref.1), custom_call_target="tpu_custom_call" | custom-call | tf_op jit(solution)/shard_map/attend_project/pallas_call | solution.py:212
  37.4 0.0 copy-start.5
  37.4 0.0 copy-start.7
  37.4 0.0 copy-start.6
  37.4 0.0 copy-start.2
  37.4 0.0 reduce-scatter.2.cloned.1.call-update
  37.5 0.6 copy-done.5
  38.1 0.0 copy-done.7
  38.1 0.0 copy-done.6
  38.1 0.1 copy.18
  38.3 31.5 %reduce-scatter.2.cloned.1.call-done = bf16[128,2048]{1,0:T(8,128)(2,1)} async-done(((bf16[512,2048]{1,0:T(8,128)(2,1)}), bf16[128,2048]{1,0:T(8,128)(2,1)}) %reduce-scatter.2.cloned.1.call-update) | async-done | bytes 524304 | tf_op jit(solution)/shard_map/reduce_scatter | solution.py:634
  69.7 0.0 copy-done.2
  69.7 1.3 fusion.1
  71.1 0.0 copy-start
  71.1 0.2 fusion.3
  71.3 0.9 fusion.5.x_hbm
  72.1 0.0 copy-done
  72.1 130.4 %experts_exchange.1 = bf16[128,2048]{1,0:T(8,128)(2,1)} custom-call(bf16[128,2176]{1,0:T(8,128)(2,1)} %fusion.5.x_hbm, bf16[128,2048]{1,0:T(8,128)(2,1)} %copy-done, bf16[2048,768]{1,0:T(8,128)(2,1)} %bitcast.17, bf16[2048,768]{1,0:T(8,128)(2,1)} %bitcast.18, bf16[768,2048]{1,0:T(8,128)(2,1)} %bitcast.19), custom_call_target="tpu_custom_call" | custom-call | tf_op jit(solution)/shard_map/experts_exchange/pallas_call | solution.py:565
  202.5 1.9 copy.20
  (5 shorter events, 0.0 us)
Async XLA Ops:
  6.5 6.6 %copy-start.4 = (bf16[1,128,256]{2,1,0:T(8,128)(2,1)S(1)}, bf16[1,128,256]{2,1,0:T(8,128)(2,1)}, u32[]{:S(2)}) copy-start(bf16[1,128,256]{2,1,0:T(8,128)(2,1)} %param.12) | copy-start | bytes 196612
  6.5 6.6 %copy-start.3 = (bf16[1,128,256]{2,1,0:T(8,128)(2,1)S(1)}, bf16[1,128,256]{2,1,0:T(8,128)(2,1)}, u32[]{:S(2)}) copy-start(bf16[1,128,256]{2,1,0:T(8,128)(2,1)} %param.13) | copy-start | bytes 196612
  8.9 17.5 %all-to-all-start = ((bf16[128,4,512]{2,0,1:T(8,128)(2,1)}), bf16[128,4,512]{2,0,1:T(8,128)(2,1)S(1)}, u32[]{:S(2)}, u32[]{:S(2)}) async-start(bf16[128,4,512]{2,0,1:T(8,128)(2,1)} %copy.17), calls=%async_computation | async-start | bytes 1048576 | tf_op jit(solution)/shard_map/all_to_all | solution.py:626
  13.2 56.6 %reduce-scatter.2.cloned.1.call-start = ((), (), s32[]{:S(2)}) async-start(), calls=%async_computation.2 | async-start | bytes 2621440 | tf_op jit(solution)/shard_map/reduce_scatter | solution.py:634
  26.4 0.8 copy-start.1
  37.4 0.7 copy-start.5
  37.4 0.7 copy-start.7
  37.4 0.7 copy-start.6
  37.4 32.3 %copy-start.2 = (bf16[1,128,2048]{2,1,0:T(8,128)(2,1)S(1)}, bf16[1,128,2048]{2,1,0:T(8,128)(2,1)}, u32[]{:S(2)}) copy-start(bf16[1,128,2048]{2,1,0:T(8,128)(2,1)} %param.14) | copy-start | bytes 1572868
  71.1 1.1 copy-start
Sparse Core Ops, SparseCore 0:
  37.6 32.1 reduce-scatter.1

commit v3 on v2

--- a/solution.py
+++ b/solution.py
@@ -175,55 +175,6 @@
     return (wide + mixture).astype(jnp.bfloat16)[None]
 
 
-def attend_project_kernel(heads, q_ref, k_ref, v_ref, w_ref, o_ref):
-    block = q_ref.shape[0]
-    length = k_ref.shape[0]
-    start = pl.program_id(0) * block
-    row_pos = start + lax.broadcasted_iota(jnp.int32, (block, length), 0)
-    col_pos = lax.broadcasted_iota(jnp.int32, (block, length), 1)
-    allowed = row_pos >= col_pos
-    scale = 1.0 / HD**0.5
-    outs = []
-    for head in range(heads):
-        q = q_ref[:, head * HD : (head + 1) * HD]
-        scores = (
-            lax.dot_general(
-                q, k_ref[...], (((1,), (1,)), ((), ())), preferred_element_type=jnp.float32
-            )
-            * scale
-        )
-        scores = jnp.where(allowed, scores, -1e30)
-        weights = jnp.exp(scores - jnp.max(scores, axis=1, keepdims=True))
-        total = jnp.sum(weights, axis=1, keepdims=True)
-        probs = (weights * (1.0 / total)).astype(jnp.bfloat16)
-        outs.append(
-            jnp.dot(probs, v_ref[...], preferred_element_type=jnp.float32).astype(jnp.bfloat16)
-        )
-    attended = jnp.concatenate(outs, axis=1)
-    o_ref[...] = jnp.dot(attended, w_ref[...], preferred_element_type=jnp.float32).astype(
-        o_ref.dtype
-    )
-
-
-def attend_project(queries, keys, values, weights):
-    length = queries.shape[0]
-    block = min(128, length)
-    width = queries.shape[1]
-    return pl.pallas_call(
-        functools.partial(attend_project_kernel, width // HD),
-        grid=(length // block,),
-        in_specs=[
-            pl.BlockSpec((block, width), lambda i: (i, 0)),
-            pl.BlockSpec((length, HD), lambda i: (0, 0)),
-            pl.BlockSpec((length, HD), lambda i: (0, 0)),
-            pl.BlockSpec(weights.shape, lambda i: (0, 0)),
-        ],
-        out_specs=pl.BlockSpec((block, weights.shape[1]), lambda i: (i, 0)),
-        out_shape=jax.ShapeDtypeStruct((length, weights.shape[1]), jnp.bfloat16),
-        name="attend_project",
-    )(queries, keys, values, weights)
-
-
 def nearest_order(n):
     return [sorted(range(n), key=lambda p: (abs(p - z), p)) for z in range(n)]
 
@@ -238,14 +189,34 @@
     return total
 
 
-def experts_kernel(
+def layer_kernel(
     n_sub,
-    x_hbm,
-    wide_ref,
+    q_hbm,
+    k_hbm,
+    v_hbm,
+    residual_ref,
+    proj_hbm,
+    gain_ref,
+    coeff_ref,
     wg_hbm,
     wu_hbm,
     wd_hbm,
     o_ref,
+    q_all,
+    k_all,
+    v_all,
+    proj,
+    partial,
+    core_far,
+    core_near,
+    across_near,
+    wide_ref,
+    q_send,
+    q_recv,
+    kv_send,
+    kv_recv,
+    part_send,
+    part_recv,
     rows,
     outs,
     from_core,
@@ -275,8 +246,12 @@
     z = lax.axis_index("sub")
     y = seq // 2
     c = seq % 2
-    tokens = wide_ref.shape[0]
-    width = wide_ref.shape[1]
+    tokens = residual_ref.shape[0]
+    width = residual_ref.shape[1]
+    share = q_all.shape[1]
+    heads = share // HD
+    length = q_all.shape[0]
+    group = QH // KVH
     half = tokens // 2
     order = nearest_order(n_sub)
     me = seq * n_sub + z
@@ -284,6 +259,7 @@
     low = {"sub": z - 1}
     across = {"seq": (1 - y) * 2 + c}
     partner = {"seq": y * 2 + 1 - c}
+    diagonal = {"seq": (1 - y) * 2 + 1 - c}
     has_high = z < n_sub - 1
     has_low = z > 0
 
@@ -303,19 +279,35 @@
             device_id_type=pl.DeviceIdType.MESH,
         )
 
+    def query_part(s):
+        return q_hbm.at[:, pl.ds(pl.multiple_of(s * share, share), share)]
+
+    def cache_part(ref, s):
+        return ref.at[:, pl.ds(pl.multiple_of(s * heads // group * HD, HD), HD)]
+
+    def token_rows(ref, s):
+        return ref.at[pl.ds(pl.multiple_of(s * tokens, tokens), tokens), :]
+
+    own_parts = [
+        pltpu.make_async_copy(query_part(seq), token_rows(q_all, seq), load_sem.at[0]),
+        pltpu.make_async_copy(cache_part(k_hbm, seq), token_rows(k_all, seq), load_sem.at[1]),
+        pltpu.make_async_copy(cache_part(v_hbm, seq), token_rows(v_all, seq), load_sem.at[2]),
+        pltpu.make_async_copy(proj_hbm, proj, load_sem.at[3]),
+    ]
     loads = [
-        pltpu.make_async_copy(x_hbm, rows.at[pl.ds(pl.multiple_of(slot(y, z, c) * tokens, tokens), tokens), :], load_sem.at[0]),
-        pltpu.make_async_copy(wg_hbm, wg, load_sem.at[1]),
-        pltpu.make_async_copy(wu_hbm, wu, load_sem.at[2]),
-        pltpu.make_async_copy(wd_hbm, wd, load_sem.at[3]),
+        pltpu.make_async_copy(wg_hbm, wg, load_sem.at[4]),
+        pltpu.make_async_copy(wu_hbm, wu, load_sem.at[5]),
+        pltpu.make_async_copy(wd_hbm, wd, load_sem.at[6]),
     ]
-    for load in loads:
+    for load in own_parts + loads:
         load.start()
 
     barrier = pltpu.get_barrier_semaphore()
     pl.semaphore_signal(barrier, 1, device_id=across, device_id_type=pl.DeviceIdType.MESH)
     pl.semaphore_signal(barrier, 1, device_id=partner, device_id_type=pl.DeviceIdType.MESH)
 
+    pl.semaphore_signal(barrier, 1, device_id=diagonal, device_id_type=pl.DeviceIdType.MESH)
+
     @pl.when(has_high)
     def _():
         pl.semaphore_signal(barrier, 1, device_id=high, device_id_type=pl.DeviceIdType.MESH)
@@ -324,10 +316,131 @@
     def _():
         pl.semaphore_signal(barrier, 1, device_id=low, device_id_type=pl.DeviceIdType.MESH)
 
-    peers = 2 + jnp.where(has_high, 1, 0) + jnp.where(has_low, 1, 0)
+    peers = 3 + jnp.where(has_high, 1, 0) + jnp.where(has_low, 1, 0)
     pl.semaphore_wait(barrier, peers)
 
-    loads[0].wait()
+    others = (
+        ((1 - y) * 2 + c, across),
+        ((1 - y) * 2 + 1 - c, diagonal),
+        (y * 2 + 1 - c, partner),
+    )
+
+    def scatter_copies(s, target):
+        return (
+            remote(
+                cache_part(k_hbm, s),
+                token_rows(k_all, seq),
+                kv_send.at[s],
+                kv_recv.at[seq],
+                target,
+            ),
+            remote(
+                cache_part(v_hbm, s),
+                token_rows(v_all, seq),
+                kv_send.at[4 + s],
+                kv_recv.at[4 + seq],
+                target,
+            ),
+            remote(
+                query_part(s), token_rows(q_all, seq), q_send.at[s], q_recv.at[seq], target
+            ),
+        )
+
+    for s, target in others:
+        for copy in scatter_copies(s, target):
+            copy.start()
+
+    def arrival(ref, s, sem):
+        return remote(token_rows(ref, s), token_rows(ref, s), q_send.at[s], sem, partner)
+
+    for load in own_parts:
+        load.wait()
+    for s, _ in others:
+        arrival(k_all, s, kv_recv.at[s]).wait_recv()
+        arrival(v_all, s, kv_recv.at[4 + s]).wait_recv()
+        arrival(q_all, s, q_recv.at[s]).wait_recv()
+
+    far_copy = remote(
+        token_rows(partial, (1 - y) * 2 + 1 - c), core_far, part_send.at[0], part_recv.at[0], partner
+    )
+    across_copy = remote(
+        token_rows(partial, (1 - y) * 2 + c),
+        across_near,
+        part_send.at[1],
+        part_recv.at[1],
+        across,
+    )
+    near_copy = remote(
+        token_rows(partial, y * 2 + 1 - c), core_near, part_send.at[2], part_recv.at[2], partner
+    )
+
+    def attend_step(j, carry):
+        yy = jnp.where(j < 2, 1 - y, y)
+        cc = jnp.where(j % 2 == 0, 1 - c, c)
+        i = yy * 2 + cc
+        at = pl.ds(pl.multiple_of(i * tokens, tokens), tokens)
+        row_pos = i * tokens + lax.broadcasted_iota(jnp.int32, (tokens, length), 0)
+        col_pos = lax.broadcasted_iota(jnp.int32, (tokens, length), 1)
+        allowed = row_pos >= col_pos
+        outputs = []
+        for head in range(heads):
+            scores = lax.dot_general(
+                q_all[at, head * HD : (head + 1) * HD],
+                k_all[...],
+                (((1,), (1,)), ((), ())),
+                preferred_element_type=jnp.float32,
+            ) * (1.0 / HD**0.5)
+            scores = jnp.where(allowed, scores, -1e30)
+            weights = jnp.exp(scores - jnp.max(scores, axis=1, keepdims=True))
+            total = jnp.sum(weights, axis=1, keepdims=True)
+            probs = (weights * (1.0 / total)).astype(jnp.bfloat16)
+            outputs.append(
+                jnp.dot(probs, v_all[...], preferred_element_type=jnp.float32).astype(jnp.bfloat16)
+            )
+        projected = jnp.dot(
+            jnp.concatenate(outputs, axis=1), proj[...], preferred_element_type=jnp.float32
+        )
+
+        @pl.when(j != 1)
+        def _():
+            partial[at, :] = projected.astype(jnp.bfloat16)
+
+        @pl.when(j == 0)
+        def _():
+            far_copy.start()
+
+        @pl.when(j == 1)
+        def _():
+            far_copy.wait_recv()
+            partial[at, :] = (projected + core_far[...].astype(jnp.float32)).astype(jnp.bfloat16)
+            across_copy.start()
+
+        @pl.when(j == 2)
+        def _():
+            near_copy.start()
+
+        return carry
+
+    lax.fori_loop(0, 4, attend_step, 0)
+    near_copy.wait_recv()
+    own_rows = pl.ds(pl.multiple_of(seq * tokens, tokens), tokens)
+    base = (
+        residual_ref[...].astype(jnp.float32)
+        + partial[own_rows, :].astype(jnp.float32)
+        + core_near[...].astype(jnp.float32)
+    )
+    across_copy.wait_recv()
+    hidden = (base + across_near[...].astype(jnp.float32)).astype(jnp.bfloat16)
+    wide_ref[...] = hidden
+    wide = hidden.astype(jnp.float32)
+    normed = (
+        wide
+        * lax.rsqrt(jnp.mean(wide * wide, axis=1, keepdims=True) + 1e-06)
+        * gain_ref[...].astype(jnp.float32)
+    ).astype(jnp.bfloat16)
+    own_slot = pl.ds(pl.multiple_of(slot(y, z, c) * tokens, tokens), tokens)
+    rows[own_slot, :width] = normed
+    rows[own_slot, width:] = coeff_ref[...]
 
     def row_copy(index, h, send, target):
         here = piece(rows, index, h)
@@ -381,11 +494,14 @@
         outs[at, :] = (out * coeff).astype(jnp.bfloat16)
         result_copy(yy, p).start()
 
+    for load in loads:
+        load.wait()
+
     def gather_step(k, carry):
-        t = k // 2
+        t = (k + 1) // 2
         other = k % 2
 
-        @pl.when(other == 0)
+        @pl.when(jnp.logical_or(k == 0, jnp.logical_and(other == 1, t < n_sub)))
         def _():
             p = lookup(order, z, t)
 
@@ -401,21 +517,14 @@
 
             spread(p, 1)
 
-        @pl.when(k == 0)
-        def _():
-            for load in loads[1:]:
-                load.wait()
-
-        p = lookup(order, z, t)
-
         @pl.when(other == 1)
         def _():
-            wait_rows(slot(1 - y, p, c), 0)
-            relay_copy(p, 0).start()
-            wait_rows(slot(1 - y, p, c), 1)
-            relay_copy(p, 1).start()
-
-        compute(jnp.where(other == 1, 1 - y, y), p)
+            p = lookup(order, z, t - 1)
+            for h in range(2):
+                wait_rows(slot(1 - y, p, c), h)
+                relay_copy(p, h).start()
+
+        compute(jnp.where(other == 1, 1 - y, y), lookup(order, z, t - other))
         return carry
 
     lax.fori_loop(0, 2 * n_sub, gather_step, 0)
@@ -553,22 +662,44 @@
         return carry
 
     lax.fori_loop(0, 2 * n_sub, drain, 0)
-
-
-def experts_exchange(rows_ext, hidden, w_gate, w_up, w_down, n_sub):
-    tokens, width = hidden.shape
+    for s, target in others:
+        for copy in scatter_copies(s, target):
+            copy.wait_send()
+    far_copy.wait_send()
+    across_copy.wait_send()
+    near_copy.wait_send()
+
+
+def layer(queries, keys, values, residual, proj, gain, coeffs, w_gate, w_up, w_down, n_sub):
+    tokens, width = residual.shape
+    share = proj.shape[0]
     blocks = 4 * n_sub
     dma = lambda count: pltpu.SemaphoreType.DMA((count,))
-    any_spec = pl.BlockSpec(memory_space=pl.ANY)
-    vmem_spec = pl.BlockSpec(memory_space=pltpu.VMEM)
+    hbm = pl.BlockSpec(memory_space=pl.ANY)
+    vmem = pl.BlockSpec(memory_space=pltpu.VMEM)
     bf = jnp.bfloat16
     return pl.pallas_call(
-        functools.partial(experts_kernel, n_sub),
-        in_specs=[any_spec, vmem_spec, any_spec, any_spec, any_spec],
-        out_specs=vmem_spec,
+        functools.partial(layer_kernel, n_sub),
+        in_specs=[hbm, hbm, hbm, vmem, hbm, vmem, vmem, hbm, hbm, hbm],
+        out_specs=vmem,
         out_shape=jax.ShapeDtypeStruct((tokens, width), bf),
         scratch_shapes=[
-            pltpu.VMEM((blocks * tokens, rows_ext.shape[1]), bf),
+            pltpu.VMEM((4 * tokens, share), bf),
+            pltpu.VMEM((4 * tokens, HD), bf),
+            pltpu.VMEM((4 * tokens, HD), bf),
+            pltpu.VMEM(proj.shape, bf),
+            pltpu.VMEM((4 * tokens, width), bf),
+            pltpu.VMEM((tokens, width), bf),
+            pltpu.VMEM((tokens, width), bf),
+            pltpu.VMEM((tokens, width), bf),
+            pltpu.VMEM((tokens, width), bf),
+            dma(4),
+            dma(4),
+            dma(8),
+            dma(8),
+            dma(3),
+            dma(3),
+            pltpu.VMEM((blocks * tokens, width + coeffs.shape[1]), bf),
             pltpu.VMEM((blocks * tokens, width), bf),
             pltpu.VMEM((2 * n_sub * tokens, width), bf),
             pltpu.VMEM((n_sub * tokens, width), bf),
@@ -577,7 +708,7 @@
             pltpu.VMEM(w_gate.shape, bf),
             pltpu.VMEM(w_up.shape, bf),
             pltpu.VMEM(w_down.shape, bf),
-            dma(4),
+            dma(7),
             dma(2 * blocks),
             dma(2 * n_sub),
             dma(2 * n_sub),
@@ -596,8 +727,8 @@
         compiler_params=pltpu.CompilerParams(
             collective_id=0, has_side_effects=True, vmem_limit_bytes=60 * 2**20
         ),
-        name="experts_exchange",
-    )(rows_ext, hidden, w_gate, w_up, w_down)
+        name="layer",
+    )(queries, keys, values, residual, proj, gain, coeffs, w_gate, w_up, w_down)
 
 
 def per_device_dense(
@@ -616,37 +747,25 @@
     n_seq = lax.axis_size("seq")
     n_sub = lax.axis_size("sub")
     experts = n_seq * n_sub
-    heads_here = QH // n_seq
-    group = QH // KVH
     chosen = expert_ids[0][:, :, None] == jnp.arange(experts, dtype=jnp.int32)[None, None, :]
     coeffs_local = jnp.sum(
         jnp.where(chosen, gate_weights[0].astype(jnp.float32)[:, :, None], 0.0), axis=1
     ).astype(jnp.bfloat16)
 
-    query_local = lax.all_to_all(query_rows[0], "seq", split_axis=1, concat_axis=0, tiled=True)
-    key_values = lax.all_gather(
-        jnp.concatenate([key_rows[0], value_rows[0]], axis=1), "seq", axis=0, tiled=True
-    )
-    kv_start = lax.axis_index("seq") * heads_here // group * HD
-    keys = lax.dynamic_slice_in_dim(key_values, kv_start, HD, 1)
-    values = lax.dynamic_slice_in_dim(key_values, KVH * HD + kv_start, HD, 1)
-    partial = attend_project(query_local, keys, values, out_proj)
-    projected = lax.psum_scatter(partial, "seq", scatter_dimension=0, tiled=True)
-    hidden = (residual_in[0].astype(jnp.float32) + projected.astype(jnp.float32)).astype(
-        jnp.bfloat16
-    )
-    wide = hidden.astype(jnp.float32)
-    normed = (
-        wide
-        * lax.rsqrt(jnp.mean(wide * wide, axis=1, keepdims=True) + 1e-06)
-        * norm_gain.astype(jnp.float32)
-    ).astype(jnp.bfloat16)
     lanes = 128 * ((experts + 127) // 128)
-    rows_ext = jnp.concatenate(
-        [normed, jnp.pad(coeffs_local, ((0, 0), (0, lanes - experts)))], axis=1
-    )
-    return experts_exchange(
-        rows_ext, hidden, expert_gate[0], expert_up[0], expert_down[0], n_sub
+    coeffs = jnp.pad(coeffs_local, ((0, 0), (0, lanes - experts)))
+    return layer(
+        query_rows[0],
+        key_rows[0],
+        value_rows[0],
+        residual_in[0],
+        out_proj,
+        norm_gain[None],
+        coeffs,
+        expert_gate[0],
+        expert_up[0],
+        expert_down[0],
+        n_sub,
     )[None]
 
 

time: 212 us -> 147 us (0.69)
  waiting for transfers between devices: 31.5 us -> 0 us
  between operations: 13.4 us -> 0.01 us
  blocking collectives: 12.5 us -> 0 us
  starting transfers between devices: 4.27 us -> 0 us
  local copies, waits for them, and re-layouts: 6.57 us -> 3.92 us
    reduce_scatter x1 -> x0, waiting for transfers between devices: 31.5 us -> none  [per_device_dense(): lax.psum_scatter(partial, 'seq', scatter_dimension=0, tiled=True)]
    all_gather x1 -> x0, blocking collectives: 12.5 us -> none  [per_device_dense(): lax.all_gather(jnp.concatenate([key_rows[0], value_rows[0]], axis=1), 'se...]
    all_to_all x1 -> x0, starting transfers between devices: 4.26 us -> none  [per_device_dense(): lax.all_to_all(query_rows[0], 'seq', split_axis=1, concat_axis=0, tiled=T...]
    all_to_all x2 -> x0, local copies, waits for them, and re-layouts: 2.35 us -> none  [per_device_dense(): lax.all_to_all(query_rows[0], 'seq', split_axis=1, concat_axis=0, tiled=T...]
    pallas_call x2 -> x1, Pallas kernels: 141 us -> 142 us  [layer(): pl.pallas_call(functools.partial(layer_kernel, n_sub), in_specs=[hbm, hbm...]
  transfers between devices with their start and end apart: 2 -> 0, of which waited for: 1 -> 0; matrix products, arithmetic and copies ran while one was open for 0% -> 0% of each run, Pallas kernels for 0% -> 0%
where the time goes in v3:
time: 147 us
  Pallas kernels  142 us (97%)
  local copies, waits for them, and re-layouts  3.92 us (3%)
    pallas_call x1, Pallas kernels, layer(): pl.pallas_call(functools.partial(layer_kernel, n_sub), in_specs=[hbm, hbm...  142 us

profile of v3, /device:TPU:0, one launch (start us, length us, event | category | flops | bytes accessed | tf_op | source)
XLA Modules:
  0.0 147.2 jit_solution(6018278591864855273)
XLA Ops:
  0.0 0.7 bitcast_convert_fusion
  0.7 0.7 select_reduce_fusion
  1.4 1.3 broadcast_in_dim.20.gain_ref
  2.7 0.1 copy.15
  2.8 0.6 pad.4.coeff_ref
  3.4 141.9 %layer.1 = bf16[128,2048]{1,0:T(8,128)(2,1)} custom-call(bf16[128,2048]{1,0:T(8,128)(2,1)} %bitcast.16, bf16[128,256]{1,0:T(8,128)(2,1)} %bitcast.18, bf16[128,256]{1,0:T(8,128)(2,1)} %bitcast.19, bf16[128,2048]{1,0:T(8,128)(2,1)} %bitcast.17, bf16[512,2048]{1,0:T(8,128)(2,1)} %proj_hbm.1, bf16[1,2048]{1,0:T(2,128)(2,1)} %broadcast_in_dim.20.gain_ref, ...), custom_call_target="tpu_custom_call" | custom-call | tf_op jit(solution)/shard_map/layer/pallas_call | solution.py:681
  145.3 1.9 %copy.17 = bf16[1,128,2048]{2,1,0:T(8,128)(2,1)} copy(bf16[1,128,2048]{2,1,0:T(8,128)(2,1)} %bitcast.15) | data formatting | bytes 1048576

commit v4 on v3

--- a/solution.py
+++ b/solution.py
@@ -223,6 +223,7 @@
     from_y,
     from_low,
     from_high,
+    from_mate,
     wg,
     wu,
     wd,
@@ -241,6 +242,8 @@
     high_recv,
     result_up_send,
     result_down_send,
+    mate_send,
+    mate_recv,
 ):
     seq = lax.axis_index("seq")
     z = lax.axis_index("sub")
@@ -260,6 +263,8 @@
     across = {"seq": (1 - y) * 2 + c}
     partner = {"seq": y * 2 + 1 - c}
     diagonal = {"seq": (1 - y) * 2 + 1 - c}
+    mate = z + 1 - 2 * (z % 2)
+    beside = {"sub": mate}
     has_high = z < n_sub - 1
     has_low = z > 0
 
@@ -455,7 +460,10 @@
         return (
             (jnp.logical_and(p <= z, has_high), row_copy(index, h, up_send.at[at], high)),
             (jnp.logical_and(p >= z, has_low), row_copy(index, h, down_send.at[at], low)),
-            (None, row_copy(index, h, y_send.at[at], across)),
+            (
+                jnp.logical_or(p != mate, h == 0),
+                row_copy(index, h, y_send.at[at], across),
+            ),
             (None, row_copy(index, h, core_send.at[at], partner)),
         )
 
@@ -497,9 +505,13 @@
     for load in loads:
         load.wait()
 
+    def mate_rows():
+        return row_copy(slot(1 - y, z, c), 1, mate_send.at[0], beside)
+
     def gather_step(k, carry):
         t = (k + 1) // 2
         other = k % 2
+        last = k == 2 * n_sub
 
         @pl.when(jnp.logical_or(k == 0, jnp.logical_and(other == 1, t < n_sub)))
         def _():
@@ -517,17 +529,36 @@
 
             spread(p, 1)
 
+        @pl.when(k == 2 * n_sub - 3)
+        def _():
+            mate_rows().start()
+
+        q = lookup(order, z, t - 1)
+
         @pl.when(other == 1)
         def _():
-            p = lookup(order, z, t - 1)
-            for h in range(2):
-                wait_rows(slot(1 - y, p, c), h)
-                relay_copy(p, h).start()
-
-        compute(jnp.where(other == 1, 1 - y, y), lookup(order, z, t - other))
+            wait_rows(slot(1 - y, q, c), 0)
+            relay_copy(q, 0).start()
+
+            @pl.when(q != mate)
+            def _():
+                wait_rows(slot(1 - y, q, c), 1)
+                relay_copy(q, 1).start()
+
+        @pl.when(last)
+        def _():
+            wait_rows(slot(1 - y, mate, c), 1)
+            relay_copy(mate, 1).start()
+
+        @pl.when(jnp.logical_or(other == 0, q != mate))
+        def _():
+            yy = jnp.where(jnp.logical_or(other == 1, last), 1 - y, y)
+            p = jnp.where(last, mate, jnp.where(other == 1, q, lookup(order, z, t)))
+            compute(yy, p)
+
         return carry
 
-    lax.fori_loop(0, 2 * n_sub, gather_step, 0)
+    lax.fori_loop(0, 2 * n_sub + 1, gather_step, 0)
 
     def wide_load(ref, index, h):
         at = pl.ds(pl.multiple_of(index * tokens + h * half, half), half)
@@ -559,6 +590,11 @@
         at = pl.ds(pl.multiple_of(index * tokens + h * half, half), half)
         outs[at, :] = value.astype(jnp.bfloat16)
 
+    def mate_result(p):
+        return remote(
+            piece(outs, slot(1 - y, p, c), 1), from_mate, mate_send.at[1], mate_recv.at[0], beside
+        )
+
     def y_step(k, carry):
         p = lookup(order, z, n_sub - 1 - k)
         result_copy(1 - y, p).wait_recv()
@@ -567,7 +603,15 @@
             store_out(
                 index, h, wide_load(outs, index, h) + wide_load(from_core, (1 - y) * n_sub + p, h)
             )
-            y_copy(p, h).start()
+
+            @pl.when(jnp.logical_and(p == mate, h == 1))
+            def _():
+                mate_result(mate).start()
+
+            @pl.when(jnp.logical_or(p != z, h == 0) & jnp.logical_or(p != mate, h == 0))
+            def _():
+                y_copy(p, h).start()
+
         return carry
 
     lax.fori_loop(0, n_sub, y_step, 0)
@@ -583,17 +627,27 @@
         return carry
 
     lax.fori_loop(0, n_sub, own_step, 0)
+    mate_result(z).wait_recv()
+    store_out(
+        slot(1 - y, z, c),
+        1,
+        wide_load(outs, slot(1 - y, z, c), 1) + from_mate[...].astype(jnp.float32),
+    )
+    y_copy(z, 1).start()
 
     def z_step(k, carry):
         p = lookup(order, z, n_sub - 1 - k // 2)
         h = k % 2
         index = slot(y, p, c)
-        y_copy(p, h).wait_recv()
+        direct = jnp.logical_or(p != mate, h == 0)
+
+        @pl.when(direct)
+        def _():
+            y_copy(p, h).wait_recv()
+            store_out(index, h, wide_load(outs, index, h) + wide_load(from_y, p, h))
 
         @pl.when(p > z)
         def _():
-            store_out(index, h, wide_load(outs, index, h) + wide_load(from_y, p, h))
-
             @pl.when(has_low)
             def _():
                 up_copy(p, h).wait_recv()
@@ -603,8 +657,6 @@
 
         @pl.when(p < z)
         def _():
-            store_out(index, h, wide_load(outs, index, h) + wide_load(from_y, p, h))
-
             @pl.when(has_high)
             def _():
                 down_copy(p, h).wait_recv()
@@ -615,8 +667,6 @@
         @pl.when(p == z)
         def _():
             at = pl.ds(pl.multiple_of(h * half, half), half)
-            store_out(index, h, wide_load(outs, index, h) + wide_load(from_y, p, h))
-
             @pl.when(has_low)
             def _():
                 up_copy(p, h).wait_recv()
@@ -648,7 +698,11 @@
                     copy.wait_send()
 
         relay_copy(p, h).wait_send()
-        y_copy(p, h).wait_send()
+
+        @pl.when(jnp.logical_or(p != mate, h == 0))
+        def _():
+            y_copy(p, h).wait_send()
+
         result_copy(h, p).wait_send()
 
         @pl.when(p > z)
@@ -665,6 +719,8 @@
     for s, target in others:
         for copy in scatter_copies(s, target):
             copy.wait_send()
+    mate_rows().wait_send()
+    mate_result(mate).wait_send()
     far_copy.wait_send()
     across_copy.wait_send()
     near_copy.wait_send()
@@ -705,6 +761,7 @@
             pltpu.VMEM((n_sub * tokens, width), bf),
             pltpu.VMEM((n_sub * tokens, width), bf),
             pltpu.VMEM((n_sub * tokens, width), bf),
+            pltpu.VMEM((tokens // 2, width), bf),
             pltpu.VMEM(w_gate.shape, bf),
             pltpu.VMEM(w_up.shape, bf),
             pltpu.VMEM(w_down.shape, bf),
@@ -723,6 +780,8 @@
             dma(2 * n_sub),
             dma(2 * n_sub),
             dma(2 * n_sub),
+            dma(2),
+            dma(1),
         ],
         compiler_params=pltpu.CompilerParams(
             collective_id=0, has_side_effects=True, vmem_limit_bytes=60 * 2**20
@@ -775,7 +834,7 @@
     n_seq = lax.axis_size("seq")
     experts = n_seq * lax.axis_size("sub")
     cap = max(2, (5 * tokens * topk + 4 * experts - 1) // (4 * experts))
-    if 2 * cap >= tokens and n_seq == 4:
+    if 2 * cap >= tokens and n_seq == 4 and lax.axis_size("sub") in (4, 6, 8):
         return per_device_dense(*args)
     return per_device_routed(*args)
 

time: 147 us -> 147 us (level)
  no operation moved by 1% of the time
where the time goes in v4:
time: 147 us
  Pallas kernels  142 us (97%)
  local copies, waits for them, and re-layouts  3.92 us (3%)
    pallas_call x1, Pallas kernels, layer(): pl.pallas_call(functools.partial(layer_kernel, n_sub), in_specs=[hbm, hbm...  142 us

profile of v4, /device:TPU:0, one launch (start us, length us, event | category | flops | bytes accessed | tf_op | source)
XLA Modules:
  0.0 146.9 jit_solution(9664825373951919175)
XLA Ops:
  0.0 0.7 bitcast_convert_fusion
  0.7 0.7 select_reduce_fusion
  1.4 1.3 broadcast_in_dim.20.gain_ref
  2.7 0.1 copy.15
  2.8 0.6 pad.4.coeff_ref
  3.4 141.6 %layer.1 = bf16[128,2048]{1,0:T(8,128)(2,1)} custom-call(bf16[128,2048]{1,0:T(8,128)(2,1)} %bitcast.16, bf16[128,256]{1,0:T(8,128)(2,1)} %bitcast.18, bf16[128,256]{1,0:T(8,128)(2,1)} %bitcast.19, bf16[128,2048]{1,0:T(8,128)(2,1)} %bitcast.17, bf16[512,2048]{1,0:T(8,128)(2,1)} %proj_hbm.1, bf16[1,2048]{1,0:T(2,128)(2,1)} %broadcast_in_dim.20.gain_ref, ...), custom_call_target="tpu_custom_call" | custom-call | tf_op jit(solution)/shard_map/layer/pallas_call | solution.py:737
  145.1 1.9 %copy.17 = bf16[1,128,2048]{2,1,0:T(8,128)(2,1)} copy(bf16[1,128,2048]{2,1,0:T(8,128)(2,1)} %bitcast.15) | data formatting | bytes 1048576

commit v5 on v4

--- a/solution.py
+++ b/solution.py
@@ -517,11 +517,9 @@
         def _():
             p = lookup(order, z, t)
 
-            @pl.when(t > 0)
+            @pl.when(t == 0)
             def _():
-                wait_rows(slot(y, p, c), 0)
-
-            spread(p, 0)
+                spread(p, 0)
 
             @pl.when(t > 0)
             def _():
@@ -555,6 +553,12 @@
             yy = jnp.where(jnp.logical_or(other == 1, last), 1 - y, y)
             p = jnp.where(last, mate, jnp.where(other == 1, q, lookup(order, z, t)))
             compute(yy, p)
+
+        @pl.when(jnp.logical_and(other == 0, t + 1 < n_sub))
+        def _():
+            p = lookup(order, z, t + 1)
+            wait_rows(slot(y, p, c), 0)
+            spread(p, 0)
 
         return carry
 

time: 147 us -> 147 us (level)
  no operation moved by 1% of the time
where the time goes in v5:
time: 147 us
  Pallas kernels  142 us (97%)
  local copies, waits for them, and re-layouts  3.92 us (3%)
    pallas_call x1, Pallas kernels, layer(): pl.pallas_call(functools.partial(layer_kernel, n_sub), in_specs=[hbm, hbm...  142 us

profile of v5, /device:TPU:0, one launch (start us, length us, event | category | flops | bytes accessed | tf_op | source)
XLA Modules:
  0.0 147.1 jit_solution(16504189867503198103)
XLA Ops:
  0.0 0.7 bitcast_convert_fusion
  0.7 0.7 select_reduce_fusion
  1.4 1.3 broadcast_in_dim.20.gain_ref
  2.7 0.1 copy.15
  2.8 0.6 pad.4.coeff_ref
  3.4 141.8 %layer.1 = bf16[128,2048]{1,0:T(8,128)(2,1)} custom-call(bf16[128,2048]{1,0:T(8,128)(2,1)} %bitcast.16, bf16[128,256]{1,0:T(8,128)(2,1)} %bitcast.18, bf16[128,256]{1,0:T(8,128)(2,1)} %bitcast.19, bf16[128,2048]{1,0:T(8,128)(2,1)} %bitcast.17, bf16[512,2048]{1,0:T(8,128)(2,1)} %proj_hbm.1, bf16[1,2048]{1,0:T(2,128)(2,1)} %broadcast_in_dim.20.gain_ref, ...), custom_call_target="tpu_custom_call" | custom-call | tf_op jit(solution)/shard_map/layer/pallas_call | solution.py:741
  145.2 1.9 %copy.17 = bf16[1,128,2048]{2,1,0:T(8,128)(2,1)} copy(bf16[1,128,2048]{2,1,0:T(8,128)(2,1)} %bitcast.15) | data formatting | bytes 1048576
